TPU v7x, 32 devices: a whole 2x2x4 slice. The times are simulated.
32 devices in a mesh: dp: 8 (over z, x), tp: 4 (over y, core).
Axes of the slice: x: 2, y: 2, z: 4, core: 2. Of those that a mesh axis runs over, the one named last changes fastest.
Arguments:
- inputs: bfloat16 [2, 4096, 768], P(None, 'dp'), may hold values from -6 to 6
- cotangent: bfloat16 [2, 4096, 768], P(None, 'dp'), may hold values from -6 to 6
- item_ids: int32 [2, 4096], P(None, 'dp'), may hold values from 0 to 3584, as said below
- timestep: int32 [2, 8], P(None, 'dp'), may hold values from 0 to 999
- qkv_weight: float32 [768, 3, 768], P('dp', None, 'tp'), may hold values from -0.21875 to 0.21875
- out_weight: float32 [768, 768], P('tp', 'dp'), may hold values from -0.625 to 0.625
- up_weight: float32 [768, 3072], P('dp', 'tp'), may hold values from -0.21875 to 0.21875
- down_weight: float32 [3072, 768], P('tp', 'dp'), may hold values from -0.109375 to 0.109375
- norm_params: float32 [4, 768], P(None, 'dp')
- qkv_first: float32 [768, 3, 768], P('dp', None, 'tp'), may hold values from -0.00061035156 to 0.00061035156
- out_first: float32 [768, 768], P('tp', 'dp'), may hold values from -0.00061035156 to 0.00061035156
- up_first: float32 [768, 3072], P('dp', 'tp'), may hold values from -0.00061035156 to 0.00061035156
- down_first: float32 [3072, 768], P('tp', 'dp'), may hold values from -0.00061035156 to 0.00061035156
- norm_first: float32 [4, 768], P(None, 'dp'), may hold values from -0.001953125 to 0.001953125
- qkv_second: float32 [768, 3, 768], P('dp', None, 'tp'), may hold values from 1.4122378e-10 to 5.6489513e-10
- out_second: float32 [768, 768], P('tp', 'dp'), may hold values from 1.4122378e-10 to 5.6489513e-10
- up_second: float32 [768, 3072], P('dp', 'tp'), may hold values from 1.4122378e-10 to 5.6489513e-10
- down_second: float32 [3072, 768], P('tp', 'dp'), may hold values from 1.4122378e-10 to 5.6489513e-10
- norm_second: float32 [4, 768], P(None, 'dp'), may hold values from 1.4122379e-09 to 5.6489515e-09
Outputs:
- block_out: bfloat16 [2, 4096, 768], P(None, 'dp')
- input_grad: float32 [2, 4096, 768], P(None, 'dp')
- grad_norm: float32 [], replicated
- qkv_new: float32 [768, 3, 768], P('dp', None, 'tp')
- qkv_first_new: float32 [768, 3, 768], P('dp', None, 'tp')
- qkv_second_new: float32 [768, 3, 768], P('dp', None, 'tp')
- out_new: float32 [768, 768], P('tp', 'dp')
- out_first_new: float32 [768, 768], P('tp', 'dp')
- out_second_new: float32 [768, 768], P('tp', 'dp')
- up_new: float32 [768, 3072], P('dp', 'tp')
- up_first_new: float32 [768, 3072], P('dp', 'tp')
- up_second_new: float32 [768, 3072], P('dp', 'tp')
- down_new: float32 [3072, 768], P('tp', 'dp')
- down_first_new: float32 [3072, 768], P('tp', 'dp')
- down_second_new: float32 [3072, 768], P('tp', 'dp')
- norm_new: float32 [4, 768], P(None, 'dp')
- norm_first_new: float32 [4, 768], P(None, 'dp')
- norm_second_new: float32 [4, 768], P(None, 'dp')
Inputs may be any that keep to these rules, and one draw needn't show every extreme that they name: `item_ids`: A token's id is the index, within its micro-batch, of its item's first token, so ids never decrease along a micro-batch; every block of 512 tokens of one index of dp starts a new item, so no item spans two blocks; an item has 1 to 512 tokens and in every draw some item has exactly 512.
All inputs are finite; a program needn't handle non-finite values.
Results may differ from a plain program's by a relative error of at most 0.009.
Values may be sent and summed in bfloat16 or wider, within the bound.
A program may use at most 128 MiB of HBM per device.

v0:
```python
from functools import partial
import math

import jax
import jax.numpy as jnp
from jax import lax
from jax.sharding import PartitionSpec as P

HEAD_DIM = 64
STEP = 10


norm_eps = 1e-05
clip_limit = 1.0
learn_rate = 0.02
beta_one = 0.9
beta_two = 0.999
adam_eps = 1e-08
weight_decay = 0.01


def time_embed(step_values, model_width):
    half_width = model_width // 2
    frequency = jnp.exp(
        jnp.arange(half_width, dtype=jnp.float32) * (-math.log(10000.0) / half_width)
    )
    angles = step_values.astype(jnp.float32)[..., None] * frequency
    return jnp.concatenate([jnp.sin(angles), jnp.cos(angles)], axis=-1)


def layer_norm(values, gain_row, bias_row):
    centre = values - jnp.mean(values, axis=-1, keepdims=True)
    spread = jnp.mean(centre * centre, axis=-1, keepdims=True)
    return centre * lax.rsqrt(spread + norm_eps) * gain_row + bias_row


def masked_scores(query_rows, key_rows, same_item, score_scale):
    scores = (
        jnp.einsum("thd,shd->hts", query_rows, key_rows, preferred_element_type=jnp.float32)
        * score_scale
    )
    return jnp.where(same_item, scores, -1e30)


def one_micro(gathered, stream_in, upstream, labels, embed_row):
    qkv_mat, out_mat, up_mat, down_mat, norm_rows = gathered
    tokens_here = stream_in.shape[0]
    local_width = out_mat.shape[0]
    heads_here = local_width // HEAD_DIM
    score_scale = 1.0 / math.sqrt(HEAD_DIM)
    split_shape = (tokens_here, heads_here, HEAD_DIM)
    norm_gains = norm_rows.astype(jnp.float32)
    gain_one = 1.0 + norm_gains[0]
    gain_two = 1.0 + norm_gains[2]
    stream = stream_in.astype(jnp.float32) + embed_row[None, :]
    normed_f, norm_one_back = jax.vjp(layer_norm, stream, gain_one, norm_gains[1])
    normed = normed_f.astype(jnp.bfloat16)
    triple = jnp.einsum("td,dje->jte", normed, qkv_mat, preferred_element_type=jnp.float32).astype(
        jnp.bfloat16
    )
    query_rows = triple[0].reshape(split_shape)
    key_rows = triple[1].reshape(split_shape)
    value_rows = triple[2].reshape(split_shape)
    same_item = (labels[:, None] == labels[None, :])[None]
    scores = masked_scores(query_rows, key_rows, same_item, score_scale)
    row_top = jnp.max(scores, axis=-1, keepdims=True)
    exp_scores = jnp.exp(scores - row_top)
    row_total = jnp.sum(exp_scores, axis=-1, keepdims=True)
    probs_soft = exp_scores / row_total
    log_total = row_top + jnp.log(row_total)
    context = (
        jnp.einsum(
            "hts,shd->thd",
            probs_soft.astype(jnp.bfloat16),
            value_rows,
            preferred_element_type=jnp.float32,
        )
        .reshape(tokens_here, local_width)
        .astype(jnp.bfloat16)
    )
    attn_out = lax.psum(jnp.dot(context, out_mat, preferred_element_type=jnp.float32), "tp")
    middle = stream + attn_out
    normed_two_f, norm_two_back = jax.vjp(layer_norm, middle, gain_two, norm_gains[3])
    normed_two = normed_two_f.astype(jnp.bfloat16)
    hidden_pre = jnp.dot(normed_two, up_mat, preferred_element_type=jnp.float32)
    hidden_f, gelu_back = jax.vjp(partial(jax.nn.gelu, approximate=False), hidden_pre)
    hidden = hidden_f.astype(jnp.bfloat16)
    branch = lax.psum(
        jnp.dot(hidden, down_mat, preferred_element_type=jnp.float32).astype(jnp.bfloat16), "tp"
    ).astype(jnp.float32)
    block_out = (middle + branch).astype(jnp.bfloat16)
    grad_down = jnp.einsum("tf,td->fd", hidden, upstream, preferred_element_type=jnp.float32)
    grad_hidden = jnp.einsum("td,fd->tf", upstream, down_mat, preferred_element_type=jnp.float32)
    grad_pre = gelu_back(grad_hidden)[0].astype(jnp.bfloat16)
    grad_up = jnp.einsum("td,tf->df", normed_two, grad_pre, preferred_element_type=jnp.float32)
    grad_normed_two = lax.psum(
        jnp.einsum("tf,df->td", grad_pre, up_mat, preferred_element_type=jnp.float32), "tp"
    )
    grad_middle_norm, grad_gain_two, grad_bias_two = norm_two_back(grad_normed_two)
    grad_middle = upstream.astype(jnp.float32) + grad_middle_norm
    grad_attn = grad_middle.astype(jnp.bfloat16)
    grad_outmat = jnp.einsum("tc,td->cd", context, grad_attn, preferred_element_type=jnp.float32)
    grad_context = (
        jnp.einsum("td,cd->tc", grad_attn, out_mat, preferred_element_type=jnp.float32)
        .astype(jnp.bfloat16)
        .reshape(split_shape)
    )
    probs_again = jnp.exp(masked_scores(query_rows, key_rows, same_item, score_scale) - log_total)
    grad_values = jnp.einsum(
        "hts,thd->shd",
        probs_again.astype(jnp.bfloat16),
        grad_context,
        preferred_element_type=jnp.float32,
    )
    grad_probs = jnp.einsum(
        "thd,shd->hts", grad_context, value_rows, preferred_element_type=jnp.float32
    )
    inner_sum = jnp.sum(grad_probs * probs_again, axis=-1, keepdims=True)
    grad_scores = (probs_again * (grad_probs - inner_sum)).astype(jnp.bfloat16)
    grad_query = (
        jnp.einsum("hts,shd->thd", grad_scores, key_rows, preferred_element_type=jnp.float32)
        * score_scale
    )
    grad_key = (
        jnp.einsum("hts,thd->shd", grad_scores, query_rows, preferred_element_type=jnp.float32)
        * score_scale
    )
    grad_triple = (
        jnp.stack([grad_query, grad_key, grad_values])
        .reshape(3, tokens_here, local_width)
        .astype(jnp.bfloat16)
    )
    grad_qkv = jnp.einsum("td,jte->dje", normed, grad_triple, preferred_element_type=jnp.float32)
    grad_normed = lax.psum(
        jnp.einsum("jte,dje->td", grad_triple, qkv_mat, preferred_element_type=jnp.float32).astype(
            jnp.bfloat16
        ),
        "tp",
    ).astype(jnp.float32)
    grad_stream_norm, grad_gain_one, grad_bias_one = norm_one_back(grad_normed)
    grad_input = grad_middle + grad_stream_norm
    grad_norms = jnp.stack([grad_gain_one, grad_bias_one, grad_gain_two, grad_bias_two])
    return (block_out, grad_input, (grad_qkv, grad_outmat, grad_up, grad_down, grad_norms))


def adam_step(weight, gradient, first_old, second_old):
    first_new = beta_one * first_old + (1.0 - beta_one) * gradient
    second_new = beta_two * second_old + (1.0 - beta_two) * gradient * gradient
    moment_one = first_new / (1.0 - beta_one**STEP)
    moment_two = second_new / (1.0 - beta_two**STEP)
    weight_new = weight - learn_rate * (
        moment_one / (jnp.sqrt(moment_two) + adam_eps) + weight_decay * weight
    )
    return (weight_new, first_new, second_new)


def local(
    inputs,
    cotangent,
    item_ids,
    timestep,
    qkv_weight,
    out_weight,
    up_weight,
    down_weight,
    norm_params,
    qkv_first,
    out_first,
    up_first,
    down_first,
    norm_first,
    qkv_second,
    out_second,
    up_second,
    down_second,
    norm_second,
):
    micro_count = inputs.shape[0]
    embeds = time_embed(timestep[:, 0], inputs.shape[2])
    qkv_low = qkv_weight.astype(jnp.bfloat16)
    out_low = out_weight.astype(jnp.bfloat16)
    up_low = up_weight.astype(jnp.bfloat16)
    down_low = down_weight.astype(jnp.bfloat16)
    norm_low = norm_params.astype(jnp.bfloat16)
    block_list = []
    input_list = []
    for number in range(micro_count):
        gathered = (
            lax.all_gather(qkv_low, "dp", axis=0, tiled=True),
            lax.all_gather(out_low, "dp", axis=1, tiled=True),
            lax.all_gather(up_low, "dp", axis=0, tiled=True),
            lax.all_gather(down_low, "dp", axis=1, tiled=True),
            lax.all_gather(norm_low, "dp", axis=1, tiled=True),
        )
        block_out, grad_input, grad_list = one_micro(
            gathered, inputs[number], cotangent[number], item_ids[number], embeds[number]
        )
        owned_grads = (
            lax.psum_scatter(grad_list[0], "dp", scatter_dimension=0, tiled=True),
            lax.psum_scatter(grad_list[1], "dp", scatter_dimension=1, tiled=True),
            lax.psum_scatter(grad_list[2], "dp", scatter_dimension=0, tiled=True),
            lax.psum_scatter(grad_list[3], "dp", scatter_dimension=1, tiled=True),
            lax.psum_scatter(grad_list[4], "dp", scatter_dimension=1, tiled=True),
        )
        if number == 0:
            totals = tuple(owned_grads)
        else:
            totals = tuple((left + right for left, right in zip(totals, owned_grads)))
        block_list.append(block_out)
        input_list.append(grad_input)
    own_squares = jnp.sum(totals[0] * totals[0]) + jnp.sum(totals[1] * totals[1])
    own_squares = own_squares + jnp.sum(totals[2] * totals[2]) + jnp.sum(totals[3] * totals[3])
    norm_squares = jnp.sum(totals[4] * totals[4])
    own_squares = own_squares + jnp.where(
        lax.axis_index("tp") == 0, norm_squares, jnp.zeros_like(norm_squares)
    )
    grad_norm = jnp.sqrt(lax.psum(own_squares, ("dp", "tp")))
    factor = jnp.minimum(1.0, clip_limit / (grad_norm + 1e-06))
    weights = (qkv_weight, out_weight, up_weight, down_weight, norm_params)
    firsts = (qkv_first, out_first, up_first, down_first, norm_first)
    seconds = (qkv_second, out_second, up_second, down_second, norm_second)
    result = [
        adam_step(weights[index], totals[index] * factor, firsts[index], seconds[index])
        for index in range(5)
    ]
    return (
        jnp.stack(block_list),
        jnp.stack(input_list),
        grad_norm,
        result[0][0],
        result[0][1],
        result[0][2],
        result[1][0],
        result[1][1],
        result[1][2],
        result[2][0],
        result[2][1],
        result[2][2],
        result[3][0],
        result[3][1],
        result[3][2],
        result[4][0],
        result[4][1],
        result[4][2],
    )


def solution(mesh):
    return jax.shard_map(
        local,
        mesh=mesh,
        in_specs=(
            P(None, "dp", None),
            P(None, "dp", None),
            P(None, "dp"),
            P(None, "dp"),
            P("dp", None, "tp"),
            P("tp", "dp"),
            P("dp", "tp"),
            P("tp", "dp"),
            P(None, "dp"),
            P("dp", None, "tp"),
            P("tp", "dp"),
            P("dp", "tp"),
            P("tp", "dp"),
            P(None, "dp"),
            P("dp", None, "tp"),
            P("tp", "dp"),
            P("dp", "tp"),
            P("tp", "dp"),
            P(None, "dp"),
        ),
        out_specs=(
            P(None, "dp", None),
            P(None, "dp", None),
            P(),
            P("dp", None, "tp"),
            P("dp", None, "tp"),
            P("dp", None, "tp"),
            P("tp", "dp"),
            P("tp", "dp"),
            P("tp", "dp"),
            P("dp", "tp"),
            P("dp", "tp"),
            P("dp", "tp"),
            P("tp", "dp"),
            P("tp", "dp"),
            P("tp", "dp"),
            P(None, "dp"),
            P(None, "dp"),
            P(None, "dp"),
        ),
        check_vma=False,
    )
```

profile of v0, /device:TPU:0, one launch (start us, length us, event | category | flops | bytes accessed | tf_op | source)
XLA Modules:
  0.0 724.3 jit_solution(8021237277195858394)
XLA Ops:
  9.0 1.8 fusion.30
  10.9 1.2 fusion.37
  12.2 22.2 %all-gather = bf16[8,96,4]{1,2,0:T(4,128)(2,1)S(1)} all-gather(bf16[1,96,4]{1,2,0:T(4,128)(2,1)S(1)} %convert_bitcast_fusion.2), channel_id=1, replica_groups=mesh['dp'=8,'tp'=4] {'dp'}, dimensions={0}, use_global_device_ids=true | all-gather | bytes 6912 | tf_op jit(solution)/shard_map/all_gather | solution.py:193
  35.3 35.3 %all_gather.21 = bf16[768,3,192]{2,1,0:T(4,128)(2,1)S(1)} all-gather(bf16[96,3,192]{2,1,0:T(4,128)(2,1)S(1)} %copy.82), channel_id=1, replica_groups=mesh['dp'=8,'tp'=4] {'dp'}, dimensions={0}, use_global_device_ids=true | all-gather | bytes 995328 | tf_op jit(solution)/shard_map/all_gather | solution.py:189
  70.6 2.1 copy.83
  72.6 2.0 fusion.107
  77.2 31.1 %all_gather.22 = bf16[192,768]{0,1:T(8,128)(2,1)S(1)} all-gather(bf16[192,96]{0,1:T(8,128)(2,1)S(1)} %copy.85), channel_id=1, replica_groups=mesh['dp'=8,'tp'=4] {'dp'}, dimensions={1}, use_global_device_ids=true | all-gather | bytes 331776 | tf_op jit(solution)/shard_map/all_gather | solution.py:190
  108.3 2.0 fusion.110
  114.5 1.6 fusion.133
  118.8 1.6 fusion.134
  120.4 1.6 convert_element_type.172
  122.1 1.6 convert_element_type.174
  124.0 64.7 %all-reduce.9.cloned.1.call-done = (f32[512,768]{1,0:T(8,128)}, f32[512,768]{1,0:T(8,128)}) async-done(((f32[512,768]{1,0:T(8,128)}, f32[512,768]{1,0:T(8,128)}), (f32[512,768]{1,0:T(8,128)}, f32[512,768]{1,0:T(8,128)})) %all-reduce.9.cloned.1.call-update) | async-done | bytes 3145744 | tf_op jit(solution)/shard_map/psum | solution.py:81
  188.7 3.0 fusion.123
  194.6 7.6 %multiply_convert_fusion.3 = (bf16[512,768]{1,0:T(8,128)(2,1)}, f32[512,768]{1,0:T(8,128)}, f32[512,768]{1,0:T(8,128)}) fusion(bf16[768,768]{1,0:T(8,128)(2,1)} %all-gather.4.cloned.1.call-done, f32[512,768]{1,0:T(8,128)} %copy-done.8, f32[768]{0:T(1024)} %get-tuple-element.39, f32[768]{0:T(1024)} %get-tuple-element.38, f32[512]{0:T(512)} %fusion.99, ...), kind=kOutput, calls=%fused_computation.98 | convolution fusion | flops 631504896 | bytes 6694912 | tf_op jit(solution)/shard_map/dot_general | solution.py:85
  202.2 4.3 all-gather.6.cloned.1.call-done
  206.4 3.6 add_convert_fusion.1
  211.0 2.0 fusion.135
  213.0 5.0 multiply_convert_fusion.2
  220.0 2.0 fusion.136
  222.3 1.3 log_add_fusion.1
  224.3 3.4 convolution_convert_fusion.1
  227.7 1.8 convolution_convert_fusion
  229.5 59.8 %all-reduce.7.cloned.1.call-done = (f32[512,768]{1,0:T(8,128)}, f32[512,768]{1,0:T(8,128)}) async-done(((f32[512,768]{1,0:T(8,128)}, f32[512,768]{1,0:T(8,128)}), (f32[512,768]{1,0:T(8,128)}, f32[512,768]{1,0:T(8,128)})) %all-reduce.7.cloned.1.call-update) | async-done | bytes 3145744 | tf_op jit(solution)/shard_map/psum | solution.py:96
  289.4 4.7 multiply_reduce_fusion.3
  294.2 1.4 fusion.120
  307.9 1.7 bitcast_convert_fusion.1
  309.6 1.7 bitcast_convert_fusion
  312.8 3.5 fusion.112
  319.4 61.3 %all-reduce.11.cloned.1.call-done = (bf16[512,768]{1,0:T(8,128)(2,1)}, bf16[512,768]{1,0:T(8,128)(2,1)}, bf16[512,768]{1,0:T(8,128)(2,1)}, bf16[512,768]{1,0:T(8,128)(2,1)}) async-done(((bf16[512,768]{1,0:T(8,128)(2,1)}, bf16[512,768]{1,0:T(8,128)(2,1)}, bf16[512,768]{1,0:T(8,128)(2,1)}, bf16[512,768]{1,0:T(8,128)(2,1)}), (bf16[512,768]{1,0:T(8,128)(2,1)}, bf16[512,768]{1,0:T(8,128)(2,1)}, ...) | async-done | bytes 3145744 | tf_op jit(solution)/shard_map/psum | solution.py:88
  380.7 2.5 fusion.9
  383.4 2.5 fusion.12
  387.1 4.4 convolution_add_fusion.1
  391.6 2.3 fusion.78
  394.0 2.3 convolution_add_fusion
  397.2 2.1 fusion.71
  399.4 2.5 convolution_add_fusion.2
  403.7 2.8 add_bitcast_fusion.1
  407.6 1.9 pad_maximum_fusion
  411.6 37.1 %reduce-scatter.18.cloned.1.call-done = f32[96,4]{1,0:T(8,128)} async-done(((f32[768,4]{1,0:T(8,128)}), f32[96,4]{1,0:T(8,128)}) %reduce-scatter.18.cloned.1.call-update) | async-done | bytes 1552
  450.8 69.9 %reduce-scatter.12.cloned.1.call-done = f32[96,768]{1,0:T(8,128)} async-done(((f32[768,768]{1,0:T(8,128)}), f32[96,768]{1,0:T(8,128)}) %reduce-scatter.12.cloned.1.call-update) | async-done | bytes 294928 | tf_op jit(solution)/shard_map/reduce_scatter | solution.py:201
  520.7 1.6 multiply_reduce_fusion.9
  522.4 70.6 %reduce-scatter.14.cloned.1.call-done = f32[768,96]{0,1:T(8,128)} async-done(((f32[768,768]{0,1:T(8,128)}), f32[768,96]{0,1:T(8,128)}) %reduce-scatter.14.cloned.1.call-update) | async-done | bytes 294928 | tf_op jit(solution)/shard_map/reduce_scatter | solution.py:202
  593.0 1.6 multiply_reduce_fusion.8
  594.6 70.3 %reduce-scatter.10.cloned.1.call-done = f32[96,3,192]{2,0,1:T(8,128)} async-done(((f32[768,3,192]{2,0,1:T(8,128)}), f32[96,3,192]{2,0,1:T(8,128)}) %reduce-scatter.10.cloned.1.call-update) | async-done | bytes 221200 | tf_op jit(solution)/shard_map/reduce_scatter | solution.py:199
  665.0 1.6 multiply_reduce_fusion.10
  669.3 1.3 pad_maximum_fusion.1
  670.6 39.5 %psum.71 = f32[]{:T(128)} all-reduce(f32[]{:T(128)S(6)} %add.323), channel_id=1, replica_groups=mesh['dp'=8,'tp'=4] {'dp','tp'}, use_global_device_ids=true, to_apply=%region_53.54 | all-reduce | flops 1 | bytes 8 | tf_op jit(solution)/shard_map/psum | solution.py:217
  (393 shorter events, 47.6 us)
Async XLA Ops:
  8.0 180.7 %all-reduce.9.cloned.1.call-start = ((), (), s32[]{:S(2)}) async-start(), calls=%async_computation.13 | async-start | bytes 6291456 | tf_op jit(solution)/shard_map/psum | solution.py:81
  9.0 26.1 %copy-start.38 = (f32[96,3,192]{2,0,1:T(8,128)S(1)}, f32[96,3,192]{2,0,1:T(8,128)}, u32[]{:S(2)}) copy-start(f32[96,3,192]{2,0,1:T(8,128)} %param.23) | copy-start | bytes 663556
  10.8 61.8 %copy-start.85 = (f32[512]{0:T(512)}, f32[512]{0:T(512)S(1)}, u32[]{:S(2)}) copy-start(f32[512]{0:T(512)S(1)} %get-tuple-element.109) | copy-start | bytes 6148
  10.9 97.4 %copy-start.83 = (f32[512]{0:T(512)}, f32[512]{0:T(512)S(1)}, u32[]{:S(2)}) copy-start(f32[512]{0:T(512)S(1)} %get-tuple-element.108) | copy-start | bytes 6148
  12.1 22.4 %copy-start.118 = (f32[512]{0:T(512)}, f32[512]{0:T(512)S(1)}, u32[]{:S(2)}) copy-start(f32[512]{0:T(512)S(1)} %get-tuple-element.32) | copy-start | bytes 6148
  12.1 60.5 %copy-start.104 = (f32[512]{0:T(512)}, f32[512]{0:T(512)S(1)}, u32[]{:S(2)}) copy-start(f32[512]{0:T(512)S(1)} %fusion.98) | copy-start | bytes 6148
  35.1 37.5 %copy-start.136 = (f32[768]{0:T(1024)}, f32[768]{0:T(1024)S(1)}, u32[]{:S(2)}) copy-start(f32[768]{0:T(1024)S(1)} %get-tuple-element.40) | copy-start | bytes 9220
  35.1 73.2 %copy-start.75 = (f32[768]{0:T(1024)}, f32[768]{0:T(1024)S(1)}, u32[]{:S(2)}) copy-start(f32[768]{0:T(1024)S(1)} %get-tuple-element.41) | copy-start | bytes 9220
  74.7 33.6 %copy-start.120 = (f32[512]{0:T(512)S(1)}, f32[512]{0:T(512)}, u32[]{:S(2)}) copy-start(f32[512]{0:T(512)} %get-tuple-element.33) | copy-start | bytes 6148
  75.5 35.8 %copy-start.32 = (bf16[1,512,192]{1,2,0:T(8,128)(2,1)}, bf16[1,512,192]{1,2,0:T(8,128)(2,1)S(1)}, u32[]{:S(2)}) copy-start(bf16[1,512,192]{1,2,0:T(8,128)(2,1)S(1)} %get-tuple-element.84) | copy-start | bytes 589828
  75.5 35.8 %copy-start.34 = (bf16[1,512,192]{1,2,0:T(8,128)(2,1)}, bf16[1,512,192]{1,2,0:T(8,128)(2,1)S(1)}, u32[]{:S(2)}) copy-start(bf16[1,512,192]{1,2,0:T(8,128)(2,1)S(1)} %get-tuple-element.83) | copy-start | bytes 589828
  110.5 5.5 copy-start.28
  110.5 5.5 copy-start.30
  110.6 6.7 copy-start.45
  120.4 74.2 %all-gather.4.cloned.1.call-start = ((), (), s32[]{:S(2)}) async-start(), calls=%async_computation.5 | async-start | bytes 1327104 | tf_op jit(solution)/shard_map/all_gather | solution.py:191
  122.1 84.3 %all-gather.6.cloned.1.call-start = ((), (), s32[]{:S(2)}) async-start(), calls=%async_computation.6 | async-start | bytes 1327104 | tf_op jit(solution)/shard_map/all_gather | solution.py:192
  123.8 165.5 %all-reduce.7.cloned.1.call-start = ((), (), s32[]{:S(2)}) async-start(), calls=%async_computation.12 | async-start | bytes 6291456 | tf_op jit(solution)/shard_map/psum | solution.py:96
  213.0 5.0 copy-start.12
  213.0 5.0 copy-start.141
  222.0 158.7 %all-reduce.11.cloned.1.call-start = ((), (), s32[]{:S(2)}) async-start(), calls=%async_computation.14 | async-start | bytes 6291456 | tf_op jit(solution)/shard_map/psum | solution.py:88
  297.2 5.8 copy-start.22
  301.8 5.5 copy-start.68
  311.4 4.9 copy-start.128
  311.4 4.9 copy-start.25
  311.4 4.9 copy-start.52
  311.5 90.5 %reduce-scatter.16.cloned.1.call-start = ((), (), s32[]{:S(2)}) async-start(), calls=%async_computation.10 | async-start | bytes 884736
  318.1 62.6 %copy-start.3 = (bf16[2,512,768]{2,1,0:T(8,128)(2,1)S(1)}, bf16[2,512,768]{2,1,0:T(8,128)(2,1)}, u32[]{:S(2)}) copy-start(bf16[2,512,768]{2,1,0:T(8,128)(2,1)} %param.19) | copy-start | bytes 4718596
  318.1 62.6 %copy-start.76 = (f32[768]{0:T(1024)S(1)}, f32[768]{0:T(1024)}, u32[]{:S(2)}) copy-start(f32[768]{0:T(1024)} %copy-done.75) | copy-start | bytes 9220
  318.1 62.6 %copy-start.84 = (f32[512]{0:T(512)S(1)}, f32[512]{0:T(512)}, u32[]{:S(2)}) copy-start(f32[512]{0:T(512)} %copy-done.83) | copy-start | bytes 6148
  318.1 62.6 %copy-start.86 = (f32[512]{0:T(512)S(1)}, f32[512]{0:T(512)}, u32[]{:S(2)}) copy-start(f32[512]{0:T(512)} %copy-done.85) | copy-start | bytes 6148
  319.3 129.4 %reduce-scatter.18.cloned.1.call-start = ((), (), s32[]{:S(2)}) async-start(), calls=%async_computation.11 | async-start | bytes 442368
  387.0 133.7 %reduce-scatter.12.cloned.1.call-start = ((), (), s32[]{:S(2)}) async-start(), calls=%async_computation.8 | async-start | bytes 2654208 | tf_op jit(solution)/shard_map/reduce_scatter | solution.py:201
  391.5 201.5 %reduce-scatter.14.cloned.1.call-start = ((), (), s32[]{:S(2)}) async-start(), calls=%async_computation.9 | async-start | bytes 2654208 | tf_op jit(solution)/shard_map/reduce_scatter | solution.py:202
  396.3 268.7 %reduce-scatter.10.cloned.1.call-start = ((), (), s32[]{:S(2)}) async-start(), calls=%async_computation.7 | async-start | bytes 2654208 | tf_op jit(solution)/shard_map/reduce_scatter | solution.py:199
  669.2 41.7 %copy-start.135 = (f32[4,96]{1,0:T(4,128)S(1)}, f32[4,96]{1,0:T(4,128)}, u32[]{:S(2)}) copy-start(f32[4,96]{1,0:T(4,128)} %param.27) | copy-start | bytes 4612
  669.2 41.7 %copy-start.139 = (f32[4,96]{1,0:T(4,128)S(1)}, f32[4,96]{1,0:T(4,128)}, u32[]{:S(2)}) copy-start(f32[4,96]{1,0:T(4,128)} %param.32) | copy-start | bytes 4612
  669.2 41.7 %copy-start.140 = (f32[4,96]{1,0:T(4,128)S(1)}, f32[4,96]{1,0:T(4,128)}, u32[]{:S(2)}) copy-start(f32[4,96]{1,0:T(4,128)} %param.37) | copy-start | bytes 4612
  669.2 42.3 %copy-start.59 = (f32[192,96]{1,0:T(8,128)S(1)}, f32[192,96]{1,0:T(8,128)}, u32[]{:S(2)}) copy-start(f32[192,96]{1,0:T(8,128)} %param.24) | copy-start | bytes 221188
  669.3 42.3 %copy-start.77 = (f32[192,96]{1,0:T(8,128)S(1)}, f32[192,96]{1,0:T(8,128)}, u32[]{:S(2)}) copy-start(f32[192,96]{1,0:T(8,128)} %param.29) | copy-start | bytes 221188
  669.3 42.3 %copy-start.78 = (f32[192,96]{1,0:T(8,128)S(1)}, f32[192,96]{1,0:T(8,128)}, u32[]{:S(2)}) copy-start(f32[192,96]{1,0:T(8,128)} %param.34) | copy-start | bytes 221188
  669.3 43.0 %copy-start.36 = (f32[768,96]{0,1:T(8,128)S(1)}, f32[768,96]{0,1:T(8,128)}, u32[]{:S(2)}) copy-start(f32[768,96]{0,1:T(8,128)} %param.26) | copy-start | bytes 884740
  669.3 43.0 %copy-start.41 = (f32[768,96]{0,1:T(8,128)S(1)}, f32[768,96]{0,1:T(8,128)}, u32[]{:S(2)}) copy-start(f32[768,96]{0,1:T(8,128)} %reduce-scatter.14.cloned.1.call-done) | copy-start | bytes 884740
  669.3 43.0 %copy-start.60 = (f32[768,96]{0,1:T(8,128)S(1)}, f32[768,96]{0,1:T(8,128)}, u32[]{:S(2)}) copy-start(f32[768,96]{0,1:T(8,128)} %param.31) | copy-start | bytes 884740
  669.3 43.0 %copy-start.61 = (f32[768,96]{0,1:T(8,128)S(1)}, f32[768,96]{0,1:T(8,128)}, u32[]{:S(2)}) copy-start(f32[768,96]{0,1:T(8,128)} %param.36) | copy-start | bytes 884740
  670.6 42.8 %copy-start.37 = (f32[96,768]{1,0:T(8,128)S(1)}, f32[96,768]{1,0:T(8,128)}, u32[]{:S(2)}) copy-start(f32[96,768]{1,0:T(8,128)} %param.25) | copy-start | bytes 884740
  670.6 42.8 %copy-start.40 = (f32[96,768]{1,0:T(8,128)S(1)}, f32[96,768]{1,0:T(8,128)}, u32[]{:S(2)}) copy-start(f32[96,768]{1,0:T(8,128)} %reduce-scatter.12.cloned.1.call-done) | copy-start | bytes 884740
  670.6 42.8 %copy-start.62 = (f32[96,768]{1,0:T(8,128)S(1)}, f32[96,768]{1,0:T(8,128)}, u32[]{:S(2)}) copy-start(f32[96,768]{1,0:T(8,128)} %param.30) | copy-start | bytes 884740
  670.6 42.8 %copy-start.63 = (f32[96,768]{1,0:T(8,128)S(1)}, f32[96,768]{1,0:T(8,128)}, u32[]{:S(2)}) copy-start(f32[96,768]{1,0:T(8,128)} %param.35) | copy-start | bytes 884740
  (107 other events, 260.0 us)
Sparse Core Ops, SparseCore 0:
  120.5 68.1 all-reduce.8
  222.1 67.1 all-reduce.6
  311.5 69.1 all-reduce.10
Sparse Core Ops, SparseCore 1:
  123.6 40.9 all-gather.3
  166.6 39.8 all-gather.5
  319.4 62.4 reduce-scatter.15
  387.1 61.6 reduce-scatter.17
  452.6 68.1 reduce-scatter.11
  524.7 68.3 reduce-scatter.13
  596.8 68.2 reduce-scatter.9
where the time goes:
time: 732 us; the launch traced here: 724 us
  waiting for transfers between devices  438 us (60%)
  blocking collectives  128 us (17%)
  matrix products  63.2 us (9%)
  other arithmetic  47.9 us (7%)
  local copies, waits for them, and re-layouts  22.7 us (3%)
  between operations  22.7 us (3%)
    reduce_scatter x1, waiting for transfers between devices, local(): lax.psum_scatter(grad_list[3], 'dp', scatter_dimension=1, tiled=True)  70.6 us
    reduce_scatter x1, waiting for transfers between devices, local(): lax.psum_scatter(grad_list[0], 'dp', scatter_dimension=0, tiled=True)  70.3 us
    reduce_scatter x1, waiting for transfers between devices, local(): lax.psum_scatter(grad_list[2], 'dp', scatter_dimension=0, tiled=True)  69.9 us
    psum x1, waiting for transfers between devices, one_micro(): lax.psum(jnp.dot(context, out_mat, preferred_element_type=jnp.float32), '...  64.7 us
    psum x1, waiting for transfers between devices, one_micro(): lax.psum(jnp.dot(hidden, down_mat, preferred_element_type=jnp.float32).as...  61.3 us
    psum x1, waiting for transfers between devices, one_micro(): lax.psum(jnp.einsum('tf,df->td', grad_pre, up_mat, preferred_element_type...  59.8 us
    psum x1, blocking collectives, local(): grad_norm = jnp.sqrt(lax.psum(own_squares, ('dp', 'tp')))  39.5 us
    unnamed x12, waiting for transfers between devices  37.3 us
  transfers between devices with their start and end apart: 10, of which 8 were waited for; matrix products, arithmetic and copies ran while one was open for 8% of the time, Pallas kernels for 0%

commit v1 on v0

--- a/solution.py
+++ b/solution.py
@@ -4,11 +4,12 @@
 import jax
 import jax.numpy as jnp
 from jax import lax
+from jax.experimental import pallas as pl
+from jax.experimental.pallas import tpu as pltpu
 from jax.sharding import PartitionSpec as P
 
 HEAD_DIM = 64
 STEP = 10
-
 
 norm_eps = 1e-05
 clip_limit = 1.0
@@ -18,6 +19,10 @@
 adam_eps = 1e-08
 weight_decay = 0.01
 
+BF = jnp.bfloat16
+F32 = jnp.float32
+MESH = pl.DeviceIdType.MESH
+
 
 def time_embed(step_values, model_width):
     half_width = model_width // 2
@@ -26,6 +31,510 @@
     )
     angles = step_values.astype(jnp.float32)[..., None] * frequency
     return jnp.concatenate([jnp.sin(angles), jnp.cos(angles)], axis=-1)
+
+
+def adam_step(weight, gradient, first_old, second_old):
+    first_new = beta_one * first_old + (1.0 - beta_one) * gradient
+    second_new = beta_two * second_old + (1.0 - beta_two) * gradient * gradient
+    moment_one = first_new / (1.0 - beta_one**STEP)
+    moment_two = second_new / (1.0 - beta_two**STEP)
+    weight_new = weight - learn_rate * (
+        moment_one / (jnp.sqrt(moment_two) + adam_eps) + weight_decay * weight
+    )
+    return (weight_new, first_new, second_new)
+
+
+def mm(a, b, ca, cb):
+    return lax.dot_general(a, b, (((ca,), (cb,)), ((), ())), preferred_element_type=F32)
+
+
+def layer_kernel(
+    dims,
+    x_ref, cot_ref, emb_ref, lc_ref, lr_ref, ain_ref, bin_ref, npin_ref,
+    bo_ref, ig_ref, ga_ref, gb_ref, gn_ref, gs_ref,
+    wa, wb, npg, npt, normed, qkv, probs, ctx, n2, hid, dpre, mid, dmid, bo_own, dattn, dqkv,
+    csend, crecv, own, ysend, yrecv,
+    rax_s, rax_r, rao, raz_s, raz_r,
+    rbx_s, rbx_r, rbo, rbz_s, rbz_r,
+    nacc, ncore, nsum, sqd, sqt,
+    ag_zs, ag_zr, ag_xs, ag_xr, np_s, np_r,
+    c_s, c_r, y_s, y_r, g_s, g_r, o_l,
+    rx_s, rx_r, rz_s, rz_r, nc_s, nc_r, nd_s, nd_r, qd_s, qd_r, qt_s, qt_r,
+):
+    micro, tok, width, n_dp, n_tp, heads = dims
+    n_z = n_dp // 2
+    half = tok // 2
+    own_rows = width // n_dp
+    local = heads * HEAD_DIM
+    scale = 1.0 / math.sqrt(HEAD_DIM)
+
+    dp = lax.axis_index("dp")
+    tp = lax.axis_index("tp")
+    z, xx = lax.div(dp, 2), lax.rem(dp, 2)
+    yy, cc = lax.div(tp, 2), lax.rem(tp, 2)
+    x_peer = (2 * z + 1 - xx, tp)
+    c_peer = (dp, 2 * yy + 1 - cc)
+    y_peer = (dp, 2 * (1 - yy) + cc)
+
+    def z_of(k):
+        return lax.rem(z + k, n_z)
+
+    def z_peer(k):
+        return (2 * z_of(k) + xx, tp)
+
+    def dp_of(k):
+        return lax.rem(dp + k, n_dp)
+
+    def tp_of(k):
+        return lax.rem(tp + k, n_tp)
+
+    sent = []
+
+    def copy(src, dst, s_sem, r_sem, peer):
+        return pltpu.make_async_remote_copy(
+            src_ref=src, dst_ref=dst, send_sem=s_sem, recv_sem=r_sem, device_id=peer, device_id_type=MESH
+        )
+
+    def send(src, dst, s_sem, r_sem, peer):
+        item = copy(src, dst, s_sem, r_sem, peer)
+        item.start()
+        sent.append(item)
+
+    def arrive(dst, s_sem, r_sem, peer):
+        copy(dst, dst, s_sem, r_sem, peer).wait_recv()
+
+    barrier = pltpu.get_barrier_semaphore()
+    for k in range(1, n_dp):
+        pl.semaphore_signal(barrier, inc=1, device_id=(dp_of(k), tp), device_id_type=MESH)
+    for k in range(1, n_tp):
+        pl.semaphore_signal(barrier, inc=1, device_id=(dp, tp_of(k)), device_id_type=MESH)
+    pl.semaphore_wait(barrier, n_dp + n_tp - 2)
+
+    def rows_of(j):
+        return pl.ds(pl.multiple_of(j * own_rows, own_rows), own_rows)
+
+    def half_rows(h):
+        return pl.ds(pl.multiple_of(h * half, half), half)
+
+    mine = half_rows(cc)
+    other = half_rows(1 - cc)
+
+    def ag_src(g):
+        return (ain_ref.at[pl.ds(0, 3)], ain_ref.at[3], bin_ref.at[0], bin_ref.at[1])[g]
+
+    def ag_at(g, j):
+        r = rows_of(j)
+        return (wa.at[pl.ds(0, 3), r], wa.at[3, r], wb.at[0, r], wb.at[1, r])[g]
+
+    for k in range(1, n_dp):
+        send(npin_ref, npg.at[rows_of(dp)], np_s.at[k], np_r.at[k], (dp_of(k), tp))
+    for g in range(4):
+        for k in range(1, n_z):
+            send(ag_src(g), ag_at(g, dp), ag_zs.at[g, k], ag_zr.at[g, k], z_peer(k))
+        send(ag_src(g), ag_at(g, dp), ag_xs.at[g, 0], ag_xr.at[g, 0], x_peer)
+    npg[rows_of(dp), :] = npin_ref[...]
+    wa[:, rows_of(dp), :] = ain_ref[...]
+    wb[:, rows_of(dp), :] = bin_ref[...]
+
+    def ag_forward(g):
+        for k in range(1, n_z):
+            j = 2 * lax.rem(z + n_z - k, n_z) + xx
+            arrive(ag_at(g, j), ag_zs.at[g, k], ag_zr.at[g, k], z_peer(k))
+            send(ag_at(g, j), ag_at(g, j), ag_xs.at[g, k], ag_xr.at[g, k], x_peer)
+
+    def ag_finish(g):
+        for k in range(n_z):
+            j = 2 * lax.rem(z + n_z - k, n_z) + 1 - xx
+            arrive(ag_at(g, j), ag_xs.at[g, k], ag_xr.at[g, k], x_peer)
+
+    def ar_start(kind, m, part):
+        slot = kind % 2
+        csend[kind, m] = part(other).astype(BF)
+        send(csend.at[kind, m], crecv.at[kind, m], c_s.at[kind, m], c_r.at[kind, m], c_peer)
+        own[slot, m] = part(mine)
+
+    def ar_cross(kind, m):
+        arrive(crecv.at[kind, m], c_s.at[kind, m], c_r.at[kind, m], c_peer)
+        ysend[kind, m] = (own[kind % 2, m] + crecv[kind, m].astype(F32)).astype(BF)
+        send(ysend.at[kind, m], yrecv.at[kind, m], y_s.at[kind, m], y_r.at[kind, m], y_peer)
+
+    def ar_total(kind, m):
+        arrive(yrecv.at[kind, m], y_s.at[kind, m], y_r.at[kind, m], y_peer)
+        return ysend[kind, m].astype(F32) + yrecv[kind, m].astype(F32)
+
+    def share(kind, m, ref):
+        send(ref.at[m, mine], ref.at[m, mine], g_s.at[kind, m], g_r.at[kind, m], c_peer)
+
+    def shared(kind, m, ref):
+        arrive(ref.at[m, other], g_s.at[kind, m], g_r.at[kind, m], c_peer)
+
+    def centred(v):
+        c0 = v - jnp.mean(v, axis=-1, keepdims=True)
+        return c0, lax.rsqrt(jnp.mean(c0 * c0, axis=-1, keepdims=True) + norm_eps)
+
+    def norm_back(grad, hat, inv, gain):
+        dhat = grad * gain
+        return inv * (
+            dhat
+            - jnp.mean(dhat, axis=-1, keepdims=True)
+            - hat * jnp.mean(dhat * hat, axis=-1, keepdims=True)
+        )
+
+    def gain_row(i):
+        return 1.0 + npt[pl.ds(i, 1), :]
+
+    def bias_row(i):
+        return npt[pl.ds(i, 1), :]
+
+    def stream_of(m, rows):
+        return x_ref[m, rows, :].astype(F32) + emb_ref[m]
+
+    def first_norm(m):
+        c0, inv = centred(stream_of(m, pl.ds(0, tok)))
+        normed[m] = (c0 * inv * gain_row(0) + bias_row(1)).astype(BF)
+
+    def project(m):
+        for i in range(3):
+            qkv[i, m] = mm(normed[m], wa[i], 1, 0).astype(BF)
+
+    lane = lax.broadcasted_iota(jnp.int32, (1, local), 1)
+
+    def head_mask(h, value):
+        here = (lane >= h * HEAD_DIM) & (lane < (h + 1) * HEAD_DIM)
+        return jnp.where(here, value, 0.0).astype(BF)
+
+    def attend(m):
+        same = lc_ref[m] == lr_ref[m]
+        total = None
+        for h in range(heads):
+            s = mm(qkv[0, m] * head_mask(h, scale), qkv[1, m], 1, 1)
+            s = jnp.where(same, s, -1e30)
+            e = jnp.exp(s - jnp.max(s, axis=-1, keepdims=True))
+            p = e * (1.0 / jnp.sum(e, axis=-1, keepdims=True))
+            probs[m, h] = p
+            part = mm(p.astype(BF), qkv[2, m] * head_mask(h, 1.0), 1, 0)
+            total = part if total is None else total + part
+        ctx[m] = total.astype(BF)
+
+    def attn_part(m):
+        return lambda rows: mm(ctx[m, rows, :], wa[3], 1, 1)
+
+    def second_norm(m):
+        middle = stream_of(m, mine) + ar_total(0, m)
+        mid[m] = middle
+        c0, inv = centred(middle)
+        n2[m, mine, :] = (c0 * inv * gain_row(2) + bias_row(3)).astype(BF)
+        share(0, m, n2)
+
+    def feed(m):
+        shared(0, m, n2)
+        pre = mm(n2[m], wb[0], 1, 0)
+        cdf = 0.5 * (1.0 + lax.erf(pre * math.sqrt(0.5)))
+        hid[m] = (pre * cdf).astype(BF)
+        slope = cdf + pre * (jnp.exp(-0.5 * pre * pre) * (1.0 / math.sqrt(2.0 * math.pi)))
+        dpre[m] = (mm(cot_ref[m], wb[1], 1, 0) * slope).astype(BF)
+
+    def dn2_part(m):
+        return lambda rows: mm(dpre[m, rows, :], wb[0], 1, 1)
+
+    def branch_part(m):
+        return lambda rows: mm(hid[m, rows, :], wb[1], 1, 1)
+
+    def col_sum(v):
+        return jnp.sum(v, axis=0, keepdims=True)
+
+    def second_back(m):
+        grad = ar_total(1, m)
+        c0, inv = centred(mid[m])
+        hat = c0 * inv
+        nacc[m, pl.ds(0, 1), :] = col_sum(grad * hat)
+        nacc[m, pl.ds(1, 1), :] = col_sum(grad)
+        grad_middle = cot_ref[m, mine, :].astype(F32) + norm_back(grad, hat, inv, gain_row(2))
+        dmid[m] = grad_middle
+        dattn[m, mine, :] = grad_middle.astype(BF)
+        share(1, m, dattn)
+
+    def finish_block(m):
+        bo_own[m] = (mid[m] + ar_total(2, m)).astype(BF)
+        send(bo_own.at[m], bo_ref.at[m, mine], g_s.at[2, m], g_r.at[2, m], c_peer)
+        pltpu.make_async_copy(bo_own.at[m], bo_ref.at[m, mine], o_l.at[0, m]).start()
+
+    def attend_back(m):
+        shared(1, m, dattn)
+        dctx = mm(dattn[m], wa[3], 1, 0).astype(BF)
+        dq = dk = dv = None
+        for h in range(heads):
+            dch = dctx * head_mask(h, 1.0)
+            p = probs[m, h]
+            dp_ = mm(dch, qkv[2, m], 1, 1)
+            inner = jnp.sum(dp_ * p, axis=-1, keepdims=True)
+            ds = (p * (dp_ - inner)).astype(BF)
+            mask = head_mask(h, scale)
+            a = mm(ds, qkv[1, m] * mask, 1, 0)
+            b = mm(ds, qkv[0, m] * mask, 0, 0)
+            c = mm(p.astype(BF), dch, 0, 0)
+            dq = a if dq is None else dq + a
+            dk = b if dk is None else dk + b
+            dv = c if dv is None else dv + c
+        dqkv[0, m] = dq.astype(BF)
+        dqkv[1, m] = dk.astype(BF)
+        dqkv[2, m] = dv.astype(BF)
+
+    def dn1_part(m):
+        def part(rows):
+            total = mm(dqkv[0, m, rows, :], wa[0], 1, 1)
+            for i in range(1, 3):
+                total = total + mm(dqkv[i, m, rows, :], wa[i], 1, 1)
+            return total
+
+        return part
+
+    def first_back(m):
+        grad = ar_total(3, m)
+        c0, inv = centred(stream_of(m, mine))
+        hat = c0 * inv
+        nacc[m, pl.ds(2, 1), :] = col_sum(grad * hat)
+        nacc[m, pl.ds(3, 1), :] = col_sum(grad)
+        dmid[m] = dmid[m] + norm_back(grad, hat, inv, gain_row(0))
+        send(dmid.at[m], ig_ref.at[m, mine], g_s.at[3, m], g_r.at[3, m], c_peer)
+        pltpu.make_async_copy(dmid.at[m], ig_ref.at[m, mine], o_l.at[1, m]).start()
+
+    def rs_refs(g):
+        if g < 4:
+            return rax_s.at[g], rax_r.at[g], rao.at[g], raz_s.at[g], raz_r.at[g]
+        return rbx_s.at[g - 4], rbx_r.at[g - 4], rbo.at[g - 4], rbz_s.at[g - 4], rbz_r.at[g - 4]
+
+    def rs_start(g, grad):
+        xs, xr, keep, _, _ = rs_refs(g)
+        blocks = grad.reshape(n_z, 2, own_rows, grad.shape[-1])
+        left = xx == 0
+        xs[...] = jnp.where(left, blocks[:, 1], blocks[:, 0]).astype(BF)
+        send(xs, xr, rx_s.at[g], rx_r.at[g], x_peer)
+        keep[...] = jnp.where(left, blocks[:, 0], blocks[:, 1])
+
+    def rs_cross(g):
+        xs, xr, keep, zs, zr = rs_refs(g)
+        arrive(xr, rx_s.at[g], rx_r.at[g], x_peer)
+        both = keep[...] + xr[...].astype(F32)
+        keep[...] = both
+        zs[...] = both.astype(BF)
+        for k in range(1, n_z):
+            send(zs.at[z_of(k)], zr.at[k], rz_s.at[g, k], rz_r.at[g, k], z_peer(k))
+
+    def rs_finish(g):
+        _, _, keep, _, zr = rs_refs(g)
+        total = keep[z]
+        for k in range(1, n_z):
+            arrive(zr.at[k], rz_s.at[g, k], rz_r.at[g, k], z_peer(k))
+            total = total + zr[k].astype(F32)
+        if g < 4:
+            ga_ref[g] = total
+        else:
+            gb_ref[g - 4] = total
+        return jnp.sum(jnp.sum(total * total, axis=0, keepdims=True), axis=1, keepdims=True)
+
+    def flat(ref):
+        return ref[...].reshape(micro * tok, ref.shape[-1])
+
+    def norm_start(e):
+        both = nacc[0, pl.ds(2 * e, 2), :]
+        for m in range(1, micro):
+            both = both + nacc[m, pl.ds(2 * e, 2), :]
+        ncore[e, 0] = both
+        send(ncore.at[e, 0], ncore.at[e, 1], nc_s.at[e], nc_r.at[e], c_peer)
+
+    def norm_cross(e):
+        arrive(ncore.at[e, 1], nc_s.at[e], nc_r.at[e], c_peer)
+        nsum[e, dp] = ncore[e, 0] + ncore[e, 1]
+        for k in range(1, n_dp):
+            send(nsum.at[e, dp], nsum.at[e, dp], nd_s.at[e, k], nd_r.at[e, k], (dp_of(k), tp))
+
+    def norm_finish(e):
+        for k in range(1, n_dp):
+            j = lax.rem(dp + n_dp - k, n_dp)
+            arrive(nsum.at[e, j], nd_s.at[e, k], nd_r.at[e, k], (dp_of(k), tp))
+        total = nsum[e, 0]
+        for j in range(1, n_dp):
+            total = total + nsum[e, j]
+        gn_ref[e] = total
+        return jnp.sum(jnp.sum(total * total, axis=0, keepdims=True), axis=1, keepdims=True)
+
+    for k in range(1, n_dp):
+        j = lax.rem(dp + n_dp - k, n_dp)
+        arrive(npg.at[rows_of(j)], np_s.at[k], np_r.at[k], (dp_of(k), tp))
+    npt[...] = npg[...].T
+    first_norm(0)
+    first_norm(1)
+    ag_forward(0)
+    ag_finish(0)
+    project(0)
+    ag_forward(1)
+    attend(0)
+    ag_finish(1)
+    ar_start(0, 0, attn_part(0))
+    project(1)
+    ar_cross(0, 0)
+    ag_forward(2)
+    attend(1)
+    ar_start(0, 1, attn_part(1))
+    second_norm(0)
+    ag_forward(3)
+    ar_cross(0, 1)
+    ag_finish(2)
+    ag_finish(3)
+    feed(0)
+    ar_start(1, 0, dn2_part(0))
+    second_norm(1)
+    ar_cross(1, 0)
+    ar_start(2, 0, branch_part(0))
+    feed(1)
+    ar_cross(2, 0)
+    ar_start(1, 1, dn2_part(1))
+    second_back(0)
+    ar_cross(1, 1)
+    ar_start(2, 1, branch_part(1))
+    rs_start(5, mm(flat(cot_ref), flat(hid), 0, 0))
+    rs_start(4, mm(flat(n2), flat(dpre), 0, 0))
+    finish_block(0)
+    ar_cross(2, 1)
+    attend_back(0)
+    rs_cross(5)
+    ar_start(3, 0, dn1_part(0))
+    second_back(1)
+    ar_cross(3, 0)
+    norm_start(0)
+    finish_block(1)
+    attend_back(1)
+    rs_cross(4)
+    ar_start(3, 1, dn1_part(1))
+    norm_cross(0)
+    rs_start(0, mm(flat(normed), flat(dqkv.at[0]), 0, 0))
+    ar_cross(3, 1)
+    rs_start(1, mm(flat(normed), flat(dqkv.at[1]), 0, 0))
+    rs_start(2, mm(flat(normed), flat(dqkv.at[2]), 0, 0))
+    rs_start(3, mm(flat(dattn), flat(ctx), 0, 0))
+    first_back(0)
+    rs_cross(0)
+    rs_cross(1)
+    rs_cross(2)
+    rs_cross(3)
+    first_back(1)
+    norm_start(1)
+    squares = rs_finish(5) + rs_finish(4)
+    norm_cross(1)
+    for g in range(4):
+        squares = squares + rs_finish(g)
+    sqd[dp] = jnp.broadcast_to(squares, (8, 128))
+    for k in range(1, n_dp):
+        send(sqd.at[dp], sqd.at[dp], qd_s.at[k], qd_r.at[k], (dp_of(k), tp))
+    extra = norm_finish(0) + norm_finish(1)
+    for k in range(1, n_dp):
+        j = lax.rem(dp + n_dp - k, n_dp)
+        arrive(sqd.at[j], qd_s.at[k], qd_r.at[k], (dp_of(k), tp))
+    mesh_row = sqd[0]
+    for j in range(1, n_dp):
+        mesh_row = mesh_row + sqd[j]
+    sqt[tp] = mesh_row
+    for k in range(1, n_tp):
+        send(sqt.at[tp], sqt.at[tp], qt_s.at[k], qt_r.at[k], (dp, tp_of(k)))
+    for k in range(1, n_tp):
+        j = lax.rem(tp + n_tp - k, n_tp)
+        arrive(sqt.at[j], qt_s.at[k], qt_r.at[k], (dp, tp_of(k)))
+    everything = sqt[0]
+    for j in range(1, n_tp):
+        everything = everything + sqt[j]
+    gs_ref[...] = jnp.sqrt(everything + extra)
+
+    for m in range(micro):
+        arrive(bo_ref.at[m, other], g_s.at[2, m], g_r.at[2, m], c_peer)
+        arrive(ig_ref.at[m, other], g_s.at[3, m], g_r.at[3, m], c_peer)
+        pltpu.make_async_copy(bo_own.at[m], bo_ref.at[m, mine], o_l.at[0, m]).wait()
+        pltpu.make_async_copy(dmid.at[m], ig_ref.at[m, mine], o_l.at[1, m]).wait()
+    for item in sent:
+        item.wait_send()
+
+
+def layer_call(n_dp, n_tp, inputs, cotangent, item_ids, embeds, a_in, b_in, np_in):
+    micro, tok, width = inputs.shape
+    _, own_rows, local = a_in.shape
+    ff = b_in.shape[2]
+    heads = local // HEAD_DIM
+    half = tok // 2
+    n_z = n_dp // 2
+    dims = (micro, tok, width, n_dp, n_tp, heads)
+    V = pltpu.VMEM
+    DMA = pltpu.SemaphoreType.DMA
+    scratch = [
+        V((4, width, local), BF), V((2, width, ff), BF), V((width, 128), F32), V((128, width), F32),
+        V((micro, tok, width), BF), V((3, micro, tok, local), BF), V((micro, heads, tok, tok), F32),
+        V((micro, tok, local), BF), V((micro, tok, width), BF), V((micro, tok, ff), BF), V((micro, tok, ff), BF),
+        V((micro, half, width), F32), V((micro, half, width), F32), V((micro, half, width), BF),
+        V((micro, tok, width), BF), V((3, micro, tok, local), BF),
+        V((4, micro, half, width), BF), V((4, micro, half, width), BF), V((2, micro, half, width), F32),
+        V((4, micro, half, width), BF), V((4, micro, half, width), BF),
+        V((4, n_z, own_rows, local), BF), V((4, n_z, own_rows, local), BF), V((4, n_z, own_rows, local), F32),
+        V((4, n_z, own_rows, local), BF), V((4, n_z, own_rows, local), BF),
+        V((2, n_z, own_rows, ff), BF), V((2, n_z, own_rows, ff), BF), V((2, n_z, own_rows, ff), F32),
+        V((2, n_z, own_rows, ff), BF), V((2, n_z, own_rows, ff), BF),
+        V((micro, 8, width), F32), V((2, 2, 2, width), F32), V((2, n_dp, 2, width), F32),
+        V((n_dp, 8, 128), F32), V((n_tp, 8, 128), F32),
+        DMA((4, n_z)), DMA((4, n_z)), DMA((4, n_z)), DMA((4, n_z)), DMA((n_dp,)), DMA((n_dp,)),
+        DMA((4, micro)), DMA((4, micro)), DMA((4, micro)), DMA((4, micro)), DMA((4, micro)), DMA((4, micro)),
+        DMA((2, micro)),
+        DMA((6,)), DMA((6,)), DMA((6, n_z)), DMA((6, n_z)), DMA((2,)), DMA((2,)), DMA((2, n_dp)), DMA((2, n_dp)),
+        DMA((n_dp,)), DMA((n_dp,)), DMA((n_tp,)), DMA((n_tp,)),
+    ]
+    vm = pl.BlockSpec(memory_space=pltpu.VMEM)
+    anywhere = pl.BlockSpec(memory_space=pl.ANY)
+    S = jax.ShapeDtypeStruct
+    return pl.pallas_call(
+        partial(layer_kernel, dims),
+        out_shape=(
+            S((micro, tok, width), BF), S((micro, tok, width), F32),
+            S((4, own_rows, local), F32), S((2, own_rows, ff), F32), S((2, 2, width), F32), S((8, 128), F32),
+        ),
+        in_specs=[vm] * 8,
+        out_specs=(anywhere, anywhere, vm, vm, vm, vm),
+        scratch_shapes=scratch,
+        compiler_params=pltpu.CompilerParams(
+            collective_id=0, has_side_effects=True, vmem_limit_bytes=63 << 20
+        ),
+        name="layer",
+    )(
+        inputs, cotangent, embeds[:, None, :],
+        item_ids[:, :, None], item_ids[:, None, :], a_in, b_in, np_in,
+    )
+
+
+def fast_local(
+    n_dp, n_tp,
+    inputs, cotangent, item_ids, timestep, qkv_weight, out_weight, up_weight, down_weight, norm_params,
+    qkv_first, out_first, up_first, down_first, norm_first,
+    qkv_second, out_second, up_second, down_second, norm_second,
+):
+    embeds = time_embed(timestep[:, 0], inputs.shape[2])
+    a_in = jnp.concatenate(
+        [jnp.moveaxis(qkv_weight, 1, 0).astype(BF), out_weight.T[None].astype(BF)], axis=0
+    )
+    b_in = jnp.stack([up_weight.astype(BF), down_weight.T.astype(BF)])
+    np_in = jnp.pad(norm_params.astype(BF).astype(F32).T, ((0, 0), (0, 124)))
+    block_out, grad_input, ga, gb, gn, gs = layer_call(
+        n_dp, n_tp, inputs, cotangent, item_ids, embeds, a_in, b_in, np_in
+    )
+    grad_norm = gs[0, 0]
+    factor = jnp.minimum(1.0, clip_limit / (grad_norm + 1e-06))
+    own = norm_params.shape[1]
+    gnorm_rows = jnp.concatenate([gn[1], gn[0]], axis=0)
+    gnorm_own = lax.dynamic_slice_in_dim(gnorm_rows, lax.axis_index("dp") * own, own, axis=1)
+    grads = (jnp.moveaxis(ga[:3], 0, 1), ga[3].T, gb[0], gb[1].T, gnorm_own)
+    weights = (qkv_weight, out_weight, up_weight, down_weight, norm_params)
+    firsts = (qkv_first, out_first, up_first, down_first, norm_first)
+    seconds = (qkv_second, out_second, up_second, down_second, norm_second)
+    result = [
+        adam_step(weights[index], grads[index] * factor, firsts[index], seconds[index]) for index in range(5)
+    ]
+    flat = [item for triple in result for item in triple]
+    return (block_out, grad_input, grad_norm, *flat)
 
 
 def layer_norm(values, gain_row, bias_row):
@@ -141,17 +650,6 @@
     grad_input = grad_middle + grad_stream_norm
     grad_norms = jnp.stack([grad_gain_one, grad_bias_one, grad_gain_two, grad_bias_two])
     return (block_out, grad_input, (grad_qkv, grad_outmat, grad_up, grad_down, grad_norms))
-
-
-def adam_step(weight, gradient, first_old, second_old):
-    first_new = beta_one * first_old + (1.0 - beta_one) * gradient
-    second_new = beta_two * second_old + (1.0 - beta_two) * gradient * gradient
-    moment_one = first_new / (1.0 - beta_one**STEP)
-    moment_two = second_new / (1.0 - beta_two**STEP)
-    weight_new = weight - learn_rate * (
-        moment_one / (jnp.sqrt(moment_two) + adam_eps) + weight_decay * weight
-    )
-    return (weight_new, first_new, second_new)
 
 
 def local(
@@ -246,8 +744,17 @@
 
 
 def solution(mesh):
+    n_dp, n_tp = mesh.shape["dp"], mesh.shape["tp"]
+
+    def step(*args):
+        own_rows = args[4].shape[0]
+        fits = n_tp == 4 and n_dp % 2 == 0 and own_rows % 16 == 0 and args[0].shape[0] == 2
+        if fits and args[0].shape[1] % 256 == 0 and args[4].shape[2] % HEAD_DIM == 0:
+            return fast_local(n_dp, n_tp, *args)
+        return local(*args)
+
     return jax.shard_map(
-        local,
+        step,
         mesh=mesh,
         in_specs=(
             P(None, "dp", None),

time: 732 us -> 192 us (0.26); the launches traced: 724 us -> 192 us
  waiting for transfers between devices: 438 us -> 0 us
  Pallas kernels: 0 us -> 167 us
  blocking collectives: 128 us -> 0 us
  matrix products: 63.2 us -> 0 us
  other arithmetic: 47.9 us -> 11.2 us
  between operations: 22.7 us -> 1.56 us
  local copies, waits for them, and re-layouts: 22.7 us -> 12.5 us
    reduce_scatter x3 -> x0, waiting for transfers between devices: 211 us -> none  [the longest x1 70.6 us: local(): lax.psum_scatter(grad_list[3], 'dp', scatter_dimension=1, tiled=True)]
    psum x3 -> x0, waiting for transfers between devices: 186 us -> none  [the longest x1 64.7 us: one_micro(): lax.psum(jnp.dot(context, out_mat, preferred_element_type=jnp.float32), '...]
    pallas_call x0 -> x1, Pallas kernels: none -> 167 us  [layer_call(): pl.pallas_call(partial(layer_kernel, dims), out_shape=(S((micro, tok, wid...]
    all_gather x3 -> x0, blocking collectives: 88.7 us -> none  [the longest x1 35.3 us: local(): lax.all_gather(qkv_low, 'dp', axis=0, tiled=True)]
    dot_general x34 -> x0, matrix products: 59.2 us -> none  [the longest x2 12.6 us: one_micro(): hidden_pre = jnp.dot(normed_two, up_mat, preferred_element_type=jnp.float32)]
    psum x1 -> x0, blocking collectives: 39.5 us -> none  [local(): grad_norm = jnp.sqrt(lax.psum(own_squares, ('dp', 'tp')))]
    unnamed x12 -> x0, waiting for transfers between devices: 37.3 us -> none
    reduce_sum x16 -> x0, other arithmetic: 24.8 us -> none  [the longest x3 9.74 us: layer_norm(): return centre * lax.rsqrt(spread + norm_eps) * gain_row + bias_row]
  transfers between devices with their start and end apart: 10 -> 0, of which waited for: 8 -> 0; matrix products, arithmetic and copies ran while one was open for 8% -> 0% of each run, Pallas kernels for 0% -> 0%
where the time goes in v1:
time: 192 us
  Pallas kernels  167 us (87%)
  local copies, waits for them, and re-layouts  12.5 us (7%)
  other arithmetic  11.2 us (6%)
    pallas_call x1, Pallas kernels, layer_call(): pl.pallas_call(partial(layer_kernel, dims), out_shape=(S((micro, tok, wid...  167 us
    unnamed x40, local copies, waits for them, and re-layouts  7.56 us
    sub x5, other arithmetic, adam_step(): weight - learn_rate * (moment_one / (jnp.sqrt(moment_two) + adam_eps) + w...  7.19 us

profile of v1, /device:TPU:0, one launch (start us, length us, event | category | flops | bytes accessed | tf_op | source)
XLA Modules:
  0.0 192.0 jit_solution(419413041216828731)
XLA Ops:
  0.7 0.0 copy-start.4
  0.7 0.0 copy-start.3
  0.7 0.7 convert_bitcast_fusion.4
  1.4 0.1 multiply_sine_fusion
  1.5 0.6 broadcast_in_dim.12.emb_ref
  2.1 1.7 copy.48.lc_ref
  3.9 1.3 broadcast_in_dim.14.lr_ref
  5.2 1.0 copy.46
  6.2 1.0 convert_bitcast_fusion.2
  7.1 0.7 pad_maximum_fusion.1.ain_ref
  7.8 0.0 copy-done.4
  7.9 0.0 copy-done.3
  7.9 0.7 pad_maximum_fusion.bin_ref
  8.6 0.0 copy-done.12
  8.7 0.1 copy.47
  8.8 0.6 pad_convert_fusion.npin_ref
  9.4 166.7 %layer.1 = (bf16[2,512,768]{2,1,0:T(8,128)(2,1)}, f32[2,512,768]{2,1,0:T(8,128)}, f32[4,96,192]{2,1,0:T(8,128)}, f32[2,96,768]{2,1,0:T(8,128)}, f32[2,2,768]{2,1,0:T(2,128)}, /*index=5*/f32[8,128]{1,0:T(8,128)}) custom-call(bf16[2,512,768]{2,1,0:T(8,128)(2,1)} %x_ref.1, bf16[2,512,768]{2,1,0:T(8,128)(2,1)} %cot_ref.1, ...), custom_call_target="tpu_custom_call" | custom-call | tf_op jit(solution)/shard_map/layer/pallas_call | solution.py:490
  176.2 0.0 copy-start.9
  176.2 0.0 copy-start.10
  176.2 1.2 slice.21
  178.1 0.0 copy-done.2
  178.1 0.0 copy-start.5
  178.1 0.0 copy-start.6
  178.1 0.0 copy-start.7
  178.2 2.3 %multiply_subtract_fusion.2 = (f32[96,3,192]{2,0,1:T(8,128)}, f32[96,3,192]{2,0,1:T(8,128)}, f32[96,3,192]{2,0,1:T(8,128)}) fusion(f32[96,3,192]{2,0,1:T(8,128)S(1)} %copy-done.2, f32[]{:T(128)S(6)} %min.3, f32[4,96,192]{2,1,0:T(8,128)} %get-tuple-element.27, f32[96,3,192]{2,0,1:T(8,128)} %param.28, f32[96,3,192]{2,0,1:T(8,128)} %param.33), kind=kLoop, calls=%fused_computation.17 | loop fusion | flops 884736 | bytes 1548292 | tf_op jit(solution)/shard_map/sub | solution.py:41
  180.4 0.0 copy-done.9
  180.4 0.1 copy.49
  180.5 0.0 copy-done.10
  180.5 0.1 copy.50
  180.6 0.0 copy-start.8
  180.7 1.0 multiply_subtract_fusion.3
  181.7 0.7 copy.53
  182.4 0.7 copy.54
  183.2 0.7 copy.55
  183.9 0.0 copy-done.5
  183.9 0.0 copy-done.6
  183.9 0.0 copy-done.7
  183.9 1.1 multiply_subtract_fusion.1
  185.0 0.0 copy-done.8
  185.0 2.1 %multiply_subtract_fusion = (f32[768,96]{0,1:T(8,128)}, f32[768,96]{0,1:T(8,128)}, f32[768,96]{0,1:T(8,128)}) fusion(f32[768,96]{0,1:T(8,128)S(1)} %copy-done.4, f32[]{:T(128)S(6)} %min.3, f32[2,96,768]{2,1,0:T(8,128)S(1)} %copy-done.5, f32[768,96]{0,1:T(8,128)S(1)} %copy-done.8, f32[768,96]{0,1:T(8,128)} %param.36), kind=kLoop, calls=%fused_computation.13 | loop fusion | flops 1179648 | bytes 2064388 | tf_op jit(solution)/shard_map/sub | solution.py:41
  187.1 0.0 copy-done.11
  187.1 0.0 copy-done.13
  187.1 0.0 copy-done.14
  187.2 0.7 multiply_subtract_fusion.4
  187.8 0.0 copy-done.1
  187.8 1.1 copy.58
  189.0 1.3 copy-done
  190.3 1.7 copy.59
  (16 shorter events, 0.1 us)
Async XLA Ops:
  0.7 7.2 %copy-start.4 = (f32[768,96]{0,1:T(8,128)S(1)}, f32[768,96]{0,1:T(8,128)}, u32[]{:S(2)}) copy-start(f32[768,96]{0,1:T(8,128)} %param.26) | copy-start | bytes 884740
  0.7 7.2 %copy-start.3 = (f32[96,768]{1,0:T(8,128)S(1)}, f32[96,768]{1,0:T(8,128)}, u32[]{:S(2)}) copy-start(f32[96,768]{1,0:T(8,128)} %param.25) | copy-start | bytes 884740
  2.1 6.5 %copy-start.12 = (f32[4,96]{1,0:T(4,128)S(1)}, f32[4,96]{1,0:T(4,128)}, u32[]{:S(2)}) copy-start(f32[4,96]{1,0:T(4,128)} %param.27) | copy-start | bytes 4612
  9.4 168.7 %copy-start.2 = (f32[96,3,192]{2,0,1:T(8,128)S(1)}, f32[96,3,192]{2,0,1:T(8,128)}, u32[]{:S(2)}) copy-start(f32[96,3,192]{2,0,1:T(8,128)} %param.23) | copy-start | bytes 663556
  176.2 4.3 %copy-start.9 = (f32[192,96]{1,0:T(8,128)S(1)}, f32[192,96]{1,0:T(8,128)}, u32[]{:S(2)}) copy-start(f32[192,96]{1,0:T(8,128)} %param.29) | copy-start | bytes 221188
  176.2 4.4 %copy-start.10 = (f32[192,96]{1,0:T(8,128)S(1)}, f32[192,96]{1,0:T(8,128)}, u32[]{:S(2)}) copy-start(f32[192,96]{1,0:T(8,128)} %param.34) | copy-start | bytes 221188
  178.1 5.8 %copy-start.5 = (f32[2,96,768]{2,1,0:T(8,128)S(1)}, f32[2,96,768]{2,1,0:T(8,128)}, u32[]{:S(2)}) copy-start(f32[2,96,768]{2,1,0:T(8,128)} %get-tuple-element.28) | copy-start | bytes 1769476
  178.1 5.8 %copy-start.6 = (f32[96,768]{1,0:T(8,128)S(1)}, f32[96,768]{1,0:T(8,128)}, u32[]{:S(2)}) copy-start(f32[96,768]{1,0:T(8,128)} %param.30) | copy-start | bytes 884740
  178.1 5.8 %copy-start.7 = (f32[96,768]{1,0:T(8,128)S(1)}, f32[96,768]{1,0:T(8,128)}, u32[]{:S(2)}) copy-start(f32[96,768]{1,0:T(8,128)} %param.35) | copy-start | bytes 884740
  180.6 4.3 %copy-start.8 = (f32[768,96]{0,1:T(8,128)S(1)}, f32[768,96]{0,1:T(8,128)}, u32[]{:S(2)}) copy-start(f32[768,96]{0,1:T(8,128)} %param.31) | copy-start | bytes 884740
  183.9 3.2 %copy-start.11 = (f32[2,2,768]{2,1,0:T(2,128)S(1)}, f32[2,2,768]{2,1,0:T(2,128)}, u32[]{:S(2)}) copy-start(f32[2,2,768]{2,1,0:T(2,128)} %get-tuple-element.29) | copy-start | bytes 36868
  185.0 2.2 %copy-start.13 = (f32[4,96]{1,0:T(4,128)S(1)}, f32[4,96]{1,0:T(4,128)}, u32[]{:S(2)}) copy-start(f32[4,96]{1,0:T(4,128)} %param.27) | copy-start | bytes 4612
  185.0 2.2 %copy-start.14 = (f32[4,96]{1,0:T(4,128)S(1)}, f32[4,96]{1,0:T(4,128)}, u32[]{:S(2)}) copy-start(f32[4,96]{1,0:T(4,128)} %param.32) | copy-start | bytes 4612
  185.0 2.2 %copy-start.15 = (f32[4,96]{1,0:T(4,128)S(1)}, f32[4,96]{1,0:T(4,128)}, u32[]{:S(2)}) copy-start(f32[4,96]{1,0:T(4,128)} %param.37) | copy-start | bytes 4612
  185.0 2.9 %copy-start.1 = (bf16[2,512,768]{2,1,0:T(8,128)(2,1)S(1)}, bf16[2,512,768]{2,1,0:T(8,128)(2,1)}, u32[]{:S(2)}) copy-start(bf16[2,512,768]{2,1,0:T(8,128)(2,1)} %get-tuple-element.103) | copy-start | bytes 4718596
  187.8 2.5 %copy-start = (f32[2,512,768]{2,1,0:T(8,128)S(1)}, f32[2,512,768]{2,1,0:T(8,128)}, u32[]{:S(2)}) copy-start(f32[2,512,768]{2,1,0:T(8,128)} %get-tuple-element.104) | copy-start | bytes 9437188

commit v2 on v1

--- a/solution.py
+++ b/solution.py
@@ -48,16 +48,29 @@
     return lax.dot_general(a, b, (((ca,), (cb,)), ((), ())), preferred_element_type=F32)
 
 
+def fold(v):
+    cut = v.shape[-2] // 2
+    low = jnp.concatenate([v[..., :cut, 128:], v[..., cut:, 128:]], axis=-1)
+    return jnp.concatenate([v[..., :128], low], axis=-2)
+
+
+def unfold(p):
+    rows = 2 * p.shape[-2] // 3
+    low = p[..., rows:, :]
+    right = jnp.concatenate([low[..., :64], low[..., 64:]], axis=-2)
+    return jnp.concatenate([p[..., :rows, :], right], axis=-1)
+
+
 def layer_kernel(
     dims,
     x_ref, cot_ref, emb_ref, lc_ref, lr_ref, ain_ref, bin_ref, npin_ref,
-    bo_ref, ig_ref, ga_ref, gb_ref, gn_ref, gs_ref,
-    wa, wb, npg, npt, normed, qkv, probs, ctx, n2, hid, dpre, mid, dmid, bo_own, dattn, dqkv,
+    bo_ref, ig_ref, ga_ref, go_ref, gb_ref, gn_ref, gs_ref,
+    wag, wqkv, woall, wo4, wb, npg, npt,
+    normed, qkv, probs, ctx, ctxp, ctxr, n2, hid, dpre, mid, dmid, bo_own, dattn, dqkv,
     csend, crecv, own, ysend, yrecv,
-    rax_s, rax_r, rao, raz_s, raz_r,
-    rbx_s, rbx_r, rbo, rbz_s, rbz_r,
+    gfo, gfb, rax_s, rax_r, raz_s, raz_r, rbx_s, rbx_r, rbz_s, rbz_r,
     nacc, ncore, nsum, sqd, sqt,
-    ag_zs, ag_zr, ag_xs, ag_xr, np_s, np_r,
+    az_s, az_r, ax_s, ax_r, np_s, np_r, oy_s, oy_r, oc_s, oc_r, cx_s, cx_r,
     c_s, c_r, y_s, y_r, g_s, g_r, o_l,
     rx_s, rx_r, rz_s, rz_r, nc_s, nc_r, nd_s, nd_r, qd_s, qd_r, qt_s, qt_r,
 ):
@@ -65,6 +78,7 @@
     n_z = n_dp // 2
     half = tok // 2
     own_rows = width // n_dp
+    fold_rows = 3 * own_rows // 2
     local = heads * HEAD_DIM
     scale = 1.0 / math.sqrt(HEAD_DIM)
 
@@ -72,15 +86,15 @@
     tp = lax.axis_index("tp")
     z, xx = lax.div(dp, 2), lax.rem(dp, 2)
     yy, cc = lax.div(tp, 2), lax.rem(tp, 2)
+    across_tp = 2 * (1 - yy) + cc
     x_peer = (2 * z + 1 - xx, tp)
     c_peer = (dp, 2 * yy + 1 - cc)
-    y_peer = (dp, 2 * (1 - yy) + cc)
-
-    def z_of(k):
-        return lax.rem(z + k, n_z)
-
-    def z_peer(k):
-        return (2 * z_of(k) + xx, tp)
+    y_peer = (dp, across_tp)
+    d_peer = (dp, 2 * (1 - yy) + 1 - cc)
+
+    far = lax.div(z, 2)
+    column = (z + 1 - 2 * lax.rem(z, 2), 2 - far, 3 - 3 * far)
+    flip = 1 - xx
 
     def dp_of(k):
         return lax.rem(dp + k, n_dp)
@@ -120,38 +134,59 @@
     other = half_rows(1 - cc)
 
     def ag_src(g):
-        return (ain_ref.at[pl.ds(0, 3)], ain_ref.at[3], bin_ref.at[0], bin_ref.at[1])[g]
+        if g < 2:
+            return ain_ref.at[:, pl.ds(384 * g, 384 - 256 * g)]
+        return bin_ref.at[g - 2]
 
     def ag_at(g, j):
-        r = rows_of(j)
-        return (wa.at[pl.ds(0, 3), r], wa.at[3, r], wb.at[0, r], wb.at[1, r])[g]
-
-    for k in range(1, n_dp):
-        send(npin_ref, npg.at[rows_of(dp)], np_s.at[k], np_r.at[k], (dp_of(k), tp))
-    for g in range(4):
-        for k in range(1, n_z):
-            send(ag_src(g), ag_at(g, dp), ag_zs.at[g, k], ag_zr.at[g, k], z_peer(k))
-        send(ag_src(g), ag_at(g, dp), ag_xs.at[g, 0], ag_xr.at[g, 0], x_peer)
-    npg[rows_of(dp), :] = npin_ref[...]
-    wa[:, rows_of(dp), :] = ain_ref[...]
-    wb[:, rows_of(dp), :] = bin_ref[...]
-
-    def ag_forward(g):
-        for k in range(1, n_z):
-            j = 2 * lax.rem(z + n_z - k, n_z) + xx
-            arrive(ag_at(g, j), ag_zs.at[g, k], ag_zr.at[g, k], z_peer(k))
-            send(ag_at(g, j), ag_at(g, j), ag_xs.at[g, k], ag_xr.at[g, k], x_peer)
-
-    def ag_finish(g):
-        for k in range(n_z):
-            j = 2 * lax.rem(z + n_z - k, n_z) + 1 - xx
-            arrive(ag_at(g, j), ag_xs.at[g, k], ag_xr.at[g, k], x_peer)
+        if g < 2:
+            return wag.at[j, :, pl.ds(384 * g, 384 - 256 * g)]
+        return wb.at[g - 2, j]
+
+    def ag_column(g):
+        for i in range(3):
+            send(ag_src(g), ag_at(g, dp), az_s.at[g, i], az_r.at[g, z], (2 * column[i] + xx, tp))
+        ag_at(g, dp)[...] = ag_src(g)[...]
+
+    def ag_side(g):
+        send(ag_src(g), ag_at(g, dp), ax_s.at[g, 3], ax_r.at[g, z], x_peer)
+
+    def ag_pass(g, *which):
+        for i in which:
+            s = column[i]
+            block = ag_at(g, 2 * s + xx)
+            arrive(block, az_s.at[g, i], az_r.at[g, s], (2 * s + xx, tp))
+            send(block, block, ax_s.at[g, i], ax_r.at[g, s], x_peer)
+
+    def ag_done(g):
+        for i, s in enumerate((*column, z)):
+            arrive(ag_at(g, 2 * s + flip), ax_s.at[g, i], ax_r.at[g, s], x_peer)
+
+    def o_send(col, which):
+        for i in which:
+            j = 2 * (*column, z)[i] + col
+            part = ag_at(1, j)
+            send(part, woall.at[tp, j], oy_s.at[j], oy_r.at[j], y_peer)
+
+    def o_core():
+        woall[tp] = wag[:, :, 384:512]
+        send(woall.at[tp], woall.at[tp], oc_s.at[0], oc_r.at[0], c_peer)
+
+    def o_across():
+        for j in range(n_dp):
+            arrive(woall.at[across_tp, j], oy_s.at[j], oy_r.at[j], y_peer)
+        send(woall.at[across_tp], woall.at[across_tp], oc_s.at[1], oc_r.at[1], c_peer)
+
+    def o_done():
+        arrive(woall.at[2 * yy + 1 - cc], oc_s.at[0], oc_r.at[0], c_peer)
+        arrive(woall.at[2 * (1 - yy) + 1 - cc], oc_s.at[1], oc_r.at[1], c_peer)
+        for t in range(n_tp):
+            wo4[t] = unfold(woall[t]).reshape(width, local)
 
     def ar_start(kind, m, part):
-        slot = kind % 2
         csend[kind, m] = part(other).astype(BF)
         send(csend.at[kind, m], crecv.at[kind, m], c_s.at[kind, m], c_r.at[kind, m], c_peer)
-        own[slot, m] = part(mine)
+        own[kind % 2, m] = part(mine)
 
     def ar_cross(kind, m):
         arrive(crecv.at[kind, m], c_s.at[kind, m], c_r.at[kind, m], c_peer)
@@ -162,11 +197,11 @@
         arrive(yrecv.at[kind, m], y_s.at[kind, m], y_r.at[kind, m], y_peer)
         return ysend[kind, m].astype(F32) + yrecv[kind, m].astype(F32)
 
-    def share(kind, m, ref):
-        send(ref.at[m, mine], ref.at[m, mine], g_s.at[kind, m], g_r.at[kind, m], c_peer)
-
-    def shared(kind, m, ref):
-        arrive(ref.at[m, other], g_s.at[kind, m], g_r.at[kind, m], c_peer)
+    def share(i, m, ref):
+        send(ref.at[m, mine], ref.at[m, mine], g_s.at[i, m], g_r.at[i, m], c_peer)
+
+    def shared(i, m, ref):
+        arrive(ref.at[m, other], g_s.at[i, m], g_r.at[i, m], c_peer)
 
     def centred(v):
         c0 = v - jnp.mean(v, axis=-1, keepdims=True)
@@ -180,6 +215,17 @@
             - hat * jnp.mean(dhat * hat, axis=-1, keepdims=True)
         )
 
+    def open_norms():
+        block = lax.broadcasted_iota(jnp.int32, (n_dp, 128, width), 0)
+        row = lax.broadcasted_iota(jnp.int32, (n_dp, 128, width), 1)
+        col = lax.broadcasted_iota(jnp.int32, (n_dp, 128, width), 2)
+        place = ((col == block * own_rows + row) & (row < own_rows)).astype(F32).astype(BF)
+        rows = npg[0]
+        total = mm(rows, place[0], 1, 0)
+        for j in range(1, n_dp):
+            total = total + mm(npg[j], place[j], 1, 0)
+        npt[...] = total
+
     def gain_row(i):
         return 1.0 + npt[pl.ds(i, 1), :]
 
@@ -193,9 +239,13 @@
         c0, inv = centred(stream_of(m, pl.ds(0, tok)))
         normed[m] = (c0 * inv * gain_row(0) + bias_row(1)).astype(BF)
 
+    def open_qkv():
+        for i in range(3):
+            wqkv[i] = unfold(wag[:, :, 128 * i : 128 * (i + 1)]).reshape(width, local)
+
     def project(m):
         for i in range(3):
-            qkv[i, m] = mm(normed[m], wa[i], 1, 0).astype(BF)
+            qkv[i, m] = mm(normed[m], wqkv[i], 1, 0).astype(BF)
 
     lane = lax.broadcasted_iota(jnp.int32, (1, local), 1)
 
@@ -203,7 +253,7 @@
         here = (lane >= h * HEAD_DIM) & (lane < (h + 1) * HEAD_DIM)
         return jnp.where(here, value, 0.0).astype(BF)
 
-    def attend(m):
+    def attend(m, *between):
         same = lc_ref[m] == lr_ref[m]
         total = None
         for h in range(heads):
@@ -211,40 +261,53 @@
             s = jnp.where(same, s, -1e30)
             e = jnp.exp(s - jnp.max(s, axis=-1, keepdims=True))
             p = e * (1.0 / jnp.sum(e, axis=-1, keepdims=True))
-            probs[m, h] = p
+            probs[m * heads + h] = p
             part = mm(p.astype(BF), qkv[2, m] * head_mask(h, 1.0), 1, 0)
             total = part if total is None else total + part
+            for work in between[h] if h < len(between) else ():
+                work()
         ctx[m] = total.astype(BF)
-
-    def attn_part(m):
-        return lambda rows: mm(ctx[m, rows, :], wa[3], 1, 1)
+        for i in range(2):
+            ctxp[m, i] = fold(total[i * half : (i + 1) * half]).astype(BF)
+        send(ctxp.at[m, cc], ctxr.at[m, tp], cx_s.at[m, 1], cx_r.at[m, 1], y_peer)
+        send(ctxp.at[m, 1 - cc], ctxr.at[m, tp], cx_s.at[m, 2], cx_r.at[m, 2], d_peer)
+        send(ctxp.at[m, 1 - cc], ctxr.at[m, tp], cx_s.at[m, 0], cx_r.at[m, 0], c_peer)
+        ctxr[m, tp] = ctxp[m, cc]
 
     def second_norm(m):
-        middle = stream_of(m, mine) + ar_total(0, m)
+        arrive(ctxr.at[m, 2 * yy + 1 - cc], cx_s.at[m, 0], cx_r.at[m, 0], c_peer)
+        arrive(ctxr.at[m, across_tp], cx_s.at[m, 1], cx_r.at[m, 1], y_peer)
+        arrive(ctxr.at[m, 2 * (1 - yy) + 1 - cc], cx_s.at[m, 2], cx_r.at[m, 2], d_peer)
+        middle = stream_of(m, mine)
+        for t in range(n_tp):
+            middle = middle + mm(unfold(ctxr[m, t]), wo4[t], 1, 1)
         mid[m] = middle
         c0, inv = centred(middle)
         n2[m, mine, :] = (c0 * inv * gain_row(2) + bias_row(3)).astype(BF)
         share(0, m, n2)
 
+    def wide(g):
+        return wb[g].reshape(width, wb.shape[-1])
+
     def feed(m):
         shared(0, m, n2)
-        pre = mm(n2[m], wb[0], 1, 0)
+        pre = mm(n2[m], wide(0), 1, 0)
         cdf = 0.5 * (1.0 + lax.erf(pre * math.sqrt(0.5)))
         hid[m] = (pre * cdf).astype(BF)
         slope = cdf + pre * (jnp.exp(-0.5 * pre * pre) * (1.0 / math.sqrt(2.0 * math.pi)))
-        dpre[m] = (mm(cot_ref[m], wb[1], 1, 0) * slope).astype(BF)
+        dpre[m] = (mm(cot_ref[m], wide(1), 1, 0) * slope).astype(BF)
 
     def dn2_part(m):
-        return lambda rows: mm(dpre[m, rows, :], wb[0], 1, 1)
+        return lambda rows: mm(dpre[m, rows, :], wide(0), 1, 1)
 
     def branch_part(m):
-        return lambda rows: mm(hid[m, rows, :], wb[1], 1, 1)
+        return lambda rows: mm(hid[m, rows, :], wide(1), 1, 1)
 
     def col_sum(v):
         return jnp.sum(v, axis=0, keepdims=True)
 
     def second_back(m):
-        grad = ar_total(1, m)
+        grad = ar_total(0, m)
         c0, inv = centred(mid[m])
         hat = c0 * inv
         nacc[m, pl.ds(0, 1), :] = col_sum(grad * hat)
@@ -255,17 +318,18 @@
         share(1, m, dattn)
 
     def finish_block(m):
-        bo_own[m] = (mid[m] + ar_total(2, m)).astype(BF)
+        bo_own[m] = (mid[m] + ar_total(1, m)).astype(BF)
         send(bo_own.at[m], bo_ref.at[m, mine], g_s.at[2, m], g_r.at[2, m], c_peer)
         pltpu.make_async_copy(bo_own.at[m], bo_ref.at[m, mine], o_l.at[0, m]).start()
 
-    def attend_back(m):
+    def attend_back(m, *between):
         shared(1, m, dattn)
-        dctx = mm(dattn[m], wa[3], 1, 0).astype(BF)
+        wo_own = wo4[tp]
+        dctx = mm(dattn[m], wo_own, 1, 0).astype(BF)
         dq = dk = dv = None
         for h in range(heads):
             dch = dctx * head_mask(h, 1.0)
-            p = probs[m, h]
+            p = probs[m * heads + h]
             dp_ = mm(dch, qkv[2, m], 1, 1)
             inner = jnp.sum(dp_ * p, axis=-1, keepdims=True)
             ds = (p * (dp_ - inner)).astype(BF)
@@ -276,21 +340,23 @@
             dq = a if dq is None else dq + a
             dk = b if dk is None else dk + b
             dv = c if dv is None else dv + c
+            for work in between[h] if h < len(between) else ():
+                work()
         dqkv[0, m] = dq.astype(BF)
         dqkv[1, m] = dk.astype(BF)
         dqkv[2, m] = dv.astype(BF)
 
     def dn1_part(m):
         def part(rows):
-            total = mm(dqkv[0, m, rows, :], wa[0], 1, 1)
+            total = mm(dqkv[0, m, rows, :], wqkv[0], 1, 1)
             for i in range(1, 3):
-                total = total + mm(dqkv[i, m, rows, :], wa[i], 1, 1)
+                total = total + mm(dqkv[i, m, rows, :], wqkv[i], 1, 1)
             return total
 
         return part
 
     def first_back(m):
-        grad = ar_total(3, m)
+        grad = ar_total(2, m)
         c0, inv = centred(stream_of(m, mine))
         hat = c0 * inv
         nacc[m, pl.ds(2, 1), :] = col_sum(grad * hat)
@@ -299,42 +365,68 @@
         send(dmid.at[m], ig_ref.at[m, mine], g_s.at[3, m], g_r.at[3, m], c_peer)
         pltpu.make_async_copy(dmid.at[m], ig_ref.at[m, mine], o_l.at[1, m]).start()
 
-    def rs_refs(g):
-        if g < 4:
-            return rax_s.at[g], rax_r.at[g], rao.at[g], raz_s.at[g], raz_r.at[g]
-        return rbx_s.at[g - 4], rbx_r.at[g - 4], rbo.at[g - 4], rbz_s.at[g - 4], rbz_r.at[g - 4]
-
-    def rs_start(g, grad):
-        xs, xr, keep, _, _ = rs_refs(g)
-        blocks = grad.reshape(n_z, 2, own_rows, grad.shape[-1])
-        left = xx == 0
-        xs[...] = jnp.where(left, blocks[:, 1], blocks[:, 0]).astype(BF)
-        send(xs, xr, rx_s.at[g], rx_r.at[g], x_peer)
-        keep[...] = jnp.where(left, blocks[:, 0], blocks[:, 1])
-
-    def rs_cross(g):
-        xs, xr, keep, zs, zr = rs_refs(g)
-        arrive(xr, rx_s.at[g], rx_r.at[g], x_peer)
-        both = keep[...] + xr[...].astype(F32)
-        keep[...] = both
-        zs[...] = both.astype(BF)
-        for k in range(1, n_z):
-            send(zs.at[z_of(k)], zr.at[k], rz_s.at[g, k], rz_r.at[g, k], z_peer(k))
-
-    def rs_finish(g):
-        _, _, keep, _, zr = rs_refs(g)
-        total = keep[z]
-        for k in range(1, n_z):
-            arrive(zr.at[k], rz_s.at[g, k], rz_r.at[g, k], z_peer(k))
-            total = total + zr[k].astype(F32)
-        if g < 4:
-            ga_ref[g] = total
-        else:
-            gb_ref[g - 4] = total
-        return jnp.sum(jnp.sum(total * total, axis=0, keepdims=True), axis=1, keepdims=True)
+    def gf(g, at, col):
+        if g == 0:
+            rows = pl.ds(pl.multiple_of(col * fold_rows, fold_rows), fold_rows)
+            return probs.at[at, rows, pl.ds(0, 384)]
+        return gfo.at[2 * at + col] if g == 1 else gfb.at[g - 2, 2 * at + col]
+
+    def rs_slots(g, at):
+        if g < 2:
+            lanes = pl.ds(384 * g, 384 - 256 * g)
+            return [r.at[at, :, lanes] for r in (rax_s, rax_r, raz_s, raz_r)]
+        return [r.at[g - 2, at] for r in (rbx_s, rbx_r, rbz_s, rbz_r)]
 
     def flat(ref):
         return ref[...].reshape(micro * tok, ref.shape[-1])
+
+    def rs_wide(g, left, right):
+        gfb[g - 2] = mm(flat(left), flat(right), 0, 0).reshape(n_dp, own_rows, right.shape[-1])
+
+    def rs_narrow(i, left, right):
+        grad = fold(mm(flat(left), flat(right), 0, 0).reshape(n_dp, own_rows, local))
+        if i == 3:
+            gfo[...] = grad
+            return
+        for j in range(n_dp):
+            rows = pl.ds((j % 2) * fold_rows, fold_rows)
+            probs[j // 2, rows, 128 * i : 128 * (i + 1)] = grad[j]
+
+    def rs_start(g):
+        for i in (2, 1, 0, 3):
+            at = (*column, z)[i]
+            here, there, _, _ = rs_slots(g, at)
+            here[...] = gf(g, at, flip)[...].astype(BF)
+            send(here, there, rx_s.at[g, i], rx_r.at[g, at], x_peer)
+
+    def rs_sum(g, i):
+        at = (*column, z)[i]
+        there = rs_slots(g, at)[1]
+        arrive(there, rx_s.at[g, i], rx_r.at[g, at], x_peer)
+        return gf(g, at, xx)[...] + there[...].astype(F32)
+
+    def rs_pass(g, *which):
+        for i in which:
+            at = column[i]
+            here = rs_slots(g, at)[2]
+            here[...] = rs_sum(g, i).astype(BF)
+            send(here, rs_slots(g, z)[3], rz_s.at[g, i], rz_r.at[g, z], (2 * at + xx, tp))
+
+    def rs_finish(g):
+        total = rs_sum(g, 3)
+        for i in range(3):
+            s = column[i]
+            there = rs_slots(g, s)[3]
+            arrive(there, rz_s.at[g, i], rz_r.at[g, s], (2 * s + xx, tp))
+            total = total + there[...].astype(F32)
+        if g == 0:
+            for i in range(3):
+                ga_ref[i] = unfold(total[:, 128 * i : 128 * (i + 1)])
+        elif g == 1:
+            go_ref[...] = unfold(total).T
+        else:
+            gb_ref[g - 2] = total
+        return jnp.sum(col_sum(total * total), axis=1, keepdims=True)
 
     def norm_start(e):
         both = nacc[0, pl.ds(2 * e, 2), :]
@@ -357,73 +449,89 @@
         for j in range(1, n_dp):
             total = total + nsum[e, j]
         gn_ref[e] = total
-        return jnp.sum(jnp.sum(total * total, axis=0, keepdims=True), axis=1, keepdims=True)
-
+        return jnp.sum(col_sum(total * total), axis=1, keepdims=True)
+
+    ag_side(0)
+    ag_column(0)
+    npg[dp] = npin_ref[...]
     for k in range(1, n_dp):
-        j = lax.rem(dp + n_dp - k, n_dp)
-        arrive(npg.at[rows_of(j)], np_s.at[k], np_r.at[k], (dp_of(k), tp))
-    npt[...] = npg[...].T
+        send(npin_ref, npg.at[dp], np_s.at[k], np_r.at[k], (dp_of(k), tp))
+    ag_column(1)
+    o_send(xx, (3,))
+    for k in range(1, n_dp):
+        arrive(npg.at[lax.rem(dp + n_dp - k, n_dp)], np_s.at[k], np_r.at[k], (dp_of(k), tp))
+    open_norms()
     first_norm(0)
+    ag_pass(0, 0)
     first_norm(1)
-    ag_forward(0)
-    ag_finish(0)
+    ag_pass(0, 1, 2)
+    ag_side(1)
+    ag_column(2)
+    ag_pass(1, 0, 1, 2)
+    o_send(xx, (0, 1, 2))
+    ag_done(0)
+    open_qkv()
     project(0)
-    ag_forward(1)
-    attend(0)
-    ag_finish(1)
-    ar_start(0, 0, attn_part(0))
+    ag_side(2)
+
+    def o_rest():
+        ag_done(1)
+        o_send(flip, (0, 1, 2, 3))
+        o_core()
+
+    attend(0, (o_rest,), (partial(ag_pass, 2, 0),), (partial(ag_pass, 2, 1), partial(ag_column, 3)))
     project(1)
+    ag_pass(2, 2)
+    ag_side(3)
+    attend(1, (o_across,), (partial(ag_pass, 3, 0),), (partial(ag_pass, 3, 1),))
+    o_done()
+    second_norm(0)
+    ag_done(2)
+    ag_pass(3, 2)
+    second_norm(1)
+    ag_done(3)
+    feed(0)
+    ar_start(0, 0, dn2_part(0))
+    feed(1)
     ar_cross(0, 0)
-    ag_forward(2)
-    attend(1)
-    ar_start(0, 1, attn_part(1))
-    second_norm(0)
-    ag_forward(3)
+    ar_start(0, 1, dn2_part(1))
+    rs_wide(3, cot_ref, hid)
     ar_cross(0, 1)
-    ag_finish(2)
-    ag_finish(3)
-    feed(0)
-    ar_start(1, 0, dn2_part(0))
-    second_norm(1)
+    rs_start(3)
+    rs_wide(2, n2, dpre)
+    ar_start(1, 0, branch_part(0))
+    ar_start(1, 1, branch_part(1))
+    second_back(0)
+    rs_pass(3, 2, 1)
+    attend_back(0, (partial(rs_pass, 3, 0),), (partial(rs_start, 2),))
+    ar_start(2, 0, dn1_part(0))
+    rs_pass(2, 2)
+    ar_cross(2, 0)
+    second_back(1)
+    rs_pass(2, 1)
+    norm_start(0)
+    attend_back(
+        1,
+        (partial(rs_pass, 2, 0), partial(rs_narrow, 3, dattn, ctx), partial(rs_start, 1)),
+        (partial(norm_cross, 0),),
+    )
+    ar_start(2, 1, dn1_part(1))
+    rs_pass(1, 2, 1, 0)
+    for i in range(3):
+        rs_narrow(i, normed, dqkv.at[i])
+    ar_cross(2, 1)
+    rs_start(0)
     ar_cross(1, 0)
-    ar_start(2, 0, branch_part(0))
-    feed(1)
-    ar_cross(2, 0)
-    ar_start(1, 1, dn2_part(1))
-    second_back(0)
     ar_cross(1, 1)
-    ar_start(2, 1, branch_part(1))
-    rs_start(5, mm(flat(cot_ref), flat(hid), 0, 0))
-    rs_start(4, mm(flat(n2), flat(dpre), 0, 0))
-    finish_block(0)
-    ar_cross(2, 1)
-    attend_back(0)
-    rs_cross(5)
-    ar_start(3, 0, dn1_part(0))
-    second_back(1)
-    ar_cross(3, 0)
-    norm_start(0)
-    finish_block(1)
-    attend_back(1)
-    rs_cross(4)
-    ar_start(3, 1, dn1_part(1))
-    norm_cross(0)
-    rs_start(0, mm(flat(normed), flat(dqkv.at[0]), 0, 0))
-    ar_cross(3, 1)
-    rs_start(1, mm(flat(normed), flat(dqkv.at[1]), 0, 0))
-    rs_start(2, mm(flat(normed), flat(dqkv.at[2]), 0, 0))
-    rs_start(3, mm(flat(dattn), flat(ctx), 0, 0))
     first_back(0)
-    rs_cross(0)
-    rs_cross(1)
-    rs_cross(2)
-    rs_cross(3)
+    rs_pass(0, 2, 1)
+    squares = rs_finish(3) + rs_finish(2)
+    squares = squares + rs_finish(1)
+    rs_pass(0, 0)
     first_back(1)
     norm_start(1)
-    squares = rs_finish(5) + rs_finish(4)
     norm_cross(1)
-    for g in range(4):
-        squares = squares + rs_finish(g)
+    squares = squares + rs_finish(0)
     sqd[dp] = jnp.broadcast_to(squares, (8, 128))
     for k in range(1, n_dp):
         send(sqd.at[dp], sqd.at[dp], qd_s.at[k], qd_r.at[k], (dp_of(k), tp))
@@ -444,7 +552,8 @@
     for j in range(1, n_tp):
         everything = everything + sqt[j]
     gs_ref[...] = jnp.sqrt(everything + extra)
-
+    finish_block(0)
+    finish_block(1)
     for m in range(micro):
         arrive(bo_ref.at[m, other], g_s.at[2, m], g_r.at[2, m], c_peer)
         arrive(ig_ref.at[m, other], g_s.at[3, m], g_r.at[3, m], c_peer)
@@ -456,32 +565,37 @@
 
 def layer_call(n_dp, n_tp, inputs, cotangent, item_ids, embeds, a_in, b_in, np_in):
     micro, tok, width = inputs.shape
-    _, own_rows, local = a_in.shape
-    ff = b_in.shape[2]
-    heads = local // HEAD_DIM
+    _, own_rows, ff = b_in.shape
+    fold_rows = a_in.shape[0]
+    heads = 2 * a_in.shape[0] * a_in.shape[1] // (8 * own_rows * HEAD_DIM)
+    local = heads * HEAD_DIM
     half = tok // 2
-    n_z = n_dp // 2
+    fold_half = 3 * half // 2
     dims = (micro, tok, width, n_dp, n_tp, heads)
     V = pltpu.VMEM
     DMA = pltpu.SemaphoreType.DMA
+    n_z = n_dp // 2
+    room = max(micro * heads, n_z)
     scratch = [
-        V((4, width, local), BF), V((2, width, ff), BF), V((width, 128), F32), V((128, width), F32),
-        V((micro, tok, width), BF), V((3, micro, tok, local), BF), V((micro, heads, tok, tok), F32),
-        V((micro, tok, local), BF), V((micro, tok, width), BF), V((micro, tok, ff), BF), V((micro, tok, ff), BF),
+        V((n_dp, fold_rows, 512), BF), V((3, width, local), BF), V((n_tp, n_dp, fold_rows, 128), BF),
+        V((n_tp, width, local), BF), V((2, n_dp, own_rows, ff), BF), V((n_dp, 8, 128), BF), V((8, width), F32),
+        V((micro, tok, width), BF), V((3, micro, tok, local), BF), V((room, tok, tok), F32),
+        V((micro, tok, local), BF), V((micro, 2, fold_half, 128), BF), V((micro, n_tp, fold_half, 128), BF),
+        V((micro, tok, width), BF), V((micro, tok, ff), BF), V((micro, tok, ff), BF),
         V((micro, half, width), F32), V((micro, half, width), F32), V((micro, half, width), BF),
         V((micro, tok, width), BF), V((3, micro, tok, local), BF),
-        V((4, micro, half, width), BF), V((4, micro, half, width), BF), V((2, micro, half, width), F32),
-        V((4, micro, half, width), BF), V((4, micro, half, width), BF),
-        V((4, n_z, own_rows, local), BF), V((4, n_z, own_rows, local), BF), V((4, n_z, own_rows, local), F32),
-        V((4, n_z, own_rows, local), BF), V((4, n_z, own_rows, local), BF),
-        V((2, n_z, own_rows, ff), BF), V((2, n_z, own_rows, ff), BF), V((2, n_z, own_rows, ff), F32),
-        V((2, n_z, own_rows, ff), BF), V((2, n_z, own_rows, ff), BF),
+        V((3, micro, half, width), BF), V((3, micro, half, width), BF), V((2, micro, half, width), F32),
+        V((3, micro, half, width), BF), V((3, micro, half, width), BF),
+        V((n_dp, fold_rows, 128), F32), V((2, n_dp, own_rows, ff), F32),
+        V((n_z, fold_rows, 512), BF), V((n_z, fold_rows, 512), BF), V((n_z, fold_rows, 512), BF), V((n_z, fold_rows, 512), BF),
+        V((2, n_z, own_rows, ff), BF), V((2, n_z, own_rows, ff), BF), V((2, n_z, own_rows, ff), BF), V((2, n_z, own_rows, ff), BF),
         V((micro, 8, width), F32), V((2, 2, 2, width), F32), V((2, n_dp, 2, width), F32),
         V((n_dp, 8, 128), F32), V((n_tp, 8, 128), F32),
-        DMA((4, n_z)), DMA((4, n_z)), DMA((4, n_z)), DMA((4, n_z)), DMA((n_dp,)), DMA((n_dp,)),
-        DMA((4, micro)), DMA((4, micro)), DMA((4, micro)), DMA((4, micro)), DMA((4, micro)), DMA((4, micro)),
+        DMA((4, n_z)), DMA((4, n_z)), DMA((4, n_z)), DMA((4, n_z)), DMA((n_dp,)), DMA((n_dp,)), DMA((n_dp,)), DMA((n_dp,)), DMA((2,)), DMA((2,)),
+        DMA((micro, 3)), DMA((micro, 3)),
+        DMA((3, micro)), DMA((3, micro)), DMA((3, micro)), DMA((3, micro)), DMA((4, micro)), DMA((4, micro)),
         DMA((2, micro)),
-        DMA((6,)), DMA((6,)), DMA((6, n_z)), DMA((6, n_z)), DMA((2,)), DMA((2,)), DMA((2, n_dp)), DMA((2, n_dp)),
+        DMA((4, n_z)), DMA((4, n_z)), DMA((4, n_z)), DMA((4, n_z)), DMA((2,)), DMA((2,)), DMA((2, n_dp)), DMA((2, n_dp)),
         DMA((n_dp,)), DMA((n_dp,)), DMA((n_tp,)), DMA((n_tp,)),
     ]
     vm = pl.BlockSpec(memory_space=pltpu.VMEM)
@@ -491,10 +605,11 @@
         partial(layer_kernel, dims),
         out_shape=(
             S((micro, tok, width), BF), S((micro, tok, width), F32),
-            S((4, own_rows, local), F32), S((2, own_rows, ff), F32), S((2, 2, width), F32), S((8, 128), F32),
+            S((3, own_rows, local), F32), S((local, own_rows), F32), S((2, own_rows, ff), F32),
+            S((2, 2, width), F32), S((8, 128), F32),
         ),
         in_specs=[vm] * 8,
-        out_specs=(anywhere, anywhere, vm, vm, vm, vm),
+        out_specs=(anywhere, anywhere, vm, vm, vm, vm, vm),
         scratch_shapes=scratch,
         compiler_params=pltpu.CompilerParams(
             collective_id=0, has_side_effects=True, vmem_limit_bytes=63 << 20
@@ -513,12 +628,11 @@
     qkv_second, out_second, up_second, down_second, norm_second,
 ):
     embeds = time_embed(timestep[:, 0], inputs.shape[2])
-    a_in = jnp.concatenate(
-        [jnp.moveaxis(qkv_weight, 1, 0).astype(BF), out_weight.T[None].astype(BF)], axis=0
-    )
+    narrow = [qkv_weight[:, i] for i in range(3)] + [out_weight.T]
+    a_in = jnp.concatenate([fold(w.astype(BF)) for w in narrow], axis=1)
     b_in = jnp.stack([up_weight.astype(BF), down_weight.T.astype(BF)])
-    np_in = jnp.pad(norm_params.astype(BF).astype(F32).T, ((0, 0), (0, 124)))
-    block_out, grad_input, ga, gb, gn, gs = layer_call(
+    np_in = jnp.pad(norm_params.astype(BF), ((0, 4), (0, 128 - norm_params.shape[1])))
+    block_out, grad_input, ga, go, gb, gn, gs = layer_call(
         n_dp, n_tp, inputs, cotangent, item_ids, embeds, a_in, b_in, np_in
     )
     grad_norm = gs[0, 0]
@@ -526,7 +640,7 @@
     own = norm_params.shape[1]
     gnorm_rows = jnp.concatenate([gn[1], gn[0]], axis=0)
     gnorm_own = lax.dynamic_slice_in_dim(gnorm_rows, lax.axis_index("dp") * own, own, axis=1)
-    grads = (jnp.moveaxis(ga[:3], 0, 1), ga[3].T, gb[0], gb[1].T, gnorm_own)
+    grads = (jnp.moveaxis(ga, 0, 1), go, gb[0], gb[1].T, gnorm_own)
     weights = (qkv_weight, out_weight, up_weight, down_weight, norm_params)
     firsts = (qkv_first, out_first, up_first, down_first, norm_first)
     seconds = (qkv_second, out_second, up_second, down_second, norm_second)
@@ -747,9 +861,10 @@
     n_dp, n_tp = mesh.shape["dp"], mesh.shape["tp"]
 
     def step(*args):
-        own_rows = args[4].shape[0]
-        fits = n_tp == 4 and n_dp % 2 == 0 and own_rows % 16 == 0 and args[0].shape[0] == 2
-        if fits and args[0].shape[1] % 256 == 0 and args[4].shape[2] % HEAD_DIM == 0:
+        micro, tok, width = args[0].shape
+        own_rows, _, local_width = args[4].shape
+        fits = n_tp == 4 and n_dp == 8 and micro == 2 and tok == 512 and own_rows == 96
+        if fits and local_width == 3 * HEAD_DIM and width % 256 == 0 and args[6].shape[1] % 256 == 0:
             return fast_local(n_dp, n_tp, *args)
         return local(*args)
 

time: 192 us -> 152 us (0.79)
  Pallas kernels: 167 us -> 130 us
  other arithmetic: 11.2 us -> 9.11 us
    pallas_call x1, Pallas kernels: 167 us -> 130 us  [layer_call(): pl.pallas_call(partial(layer_kernel, dims), out_shape=(S((micro, tok, wid...]
    unnamed x40 -> x39, local copies, waits for them, and re-layouts: 7.56 us -> 5.18 us
where the time goes in v2:
time: 152 us
  Pallas kernels  130 us (86%)
  local copies, waits for them, and re-layouts  10.7 us (7%)
  other arithmetic  9.11 us (6%)
  between operations  1.61 us (1%)
    pallas_call x1, Pallas kernels, layer_call(): pl.pallas_call(partial(layer_kernel, dims), out_shape=(S((micro, tok, wid...  130 us
    sub x5, other arithmetic, adam_step(): weight - learn_rate * (moment_one / (jnp.sqrt(moment_two) + adam_eps) + w...  5.73 us
    unnamed x39, local copies, waits for them, and re-layouts  5.18 us

profile of v2, /device:TPU:0, one launch (start us, length us, event | category | flops | bytes accessed | tf_op | source)
XLA Modules:
  0.0 151.8 jit_solution(917867659751319027)
XLA Ops:
  0.7 0.0 copy-start.4
  0.7 0.0 copy-start.3
  0.7 0.7 convert_bitcast_fusion.3
  1.4 0.1 multiply_sine_fusion
  1.5 0.6 broadcast_in_dim.11.emb_ref
  2.1 1.7 %copy.39.lc_ref = s32[2,512,1]{2,1,0:T(8,128)} copy(s32[2,512,1]{1,0,2:T(2,128)} %bitcast.48) | data formatting | bytes 8192 | tf_op jit(solution)/shard_map/broadcast_in_dim | solution.py:620
  3.9 0.0 copy-start.15
  3.9 1.3 broadcast_in_dim.13.lr_ref
  5.2 1.0 convert.5
  6.2 1.0 copy.38
  7.2 0.8 maximum_maximum_fusion.ain_ref
  8.0 0.0 copy-done.4
  8.0 0.0 copy-done.3
  8.1 0.7 pad_maximum_fusion.bin_ref
  8.8 0.0 copy-done.15
  8.8 0.6 pad.4.npin_ref
  9.4 130.4 %layer.1 = (bf16[2,512,768]{2,1,0:T(8,128)(2,1)}, f32[2,512,768]{2,1,0:T(8,128)}, f32[3,96,192]{2,1,0:T(8,128)}, f32[192,96]{1,0:T(8,128)}, f32[2,96,768]{2,1,0:...) custom-call(bf16[2,512,768]{2,1,0:T(8,128)(2,1)} %x_ref.1, bf16[2,512,768]{2,1,0:T(8,128)(2,1)} %cot_ref.1, ...), custom_call_target="tpu_custom_call" | custom-call | tf_op jit(solution)/shard_map/layer/pallas_call | solution.py:604
  139.8 0.0 copy-start.6
  139.8 0.0 copy-start.11
  139.8 0.0 copy-start.12
  139.8 0.0 copy-start.13
  139.8 0.0 copy-start.5
  139.8 0.0 copy-start.7
  139.9 0.0 copy-start.8
  139.9 1.3 slice.78
  141.9 0.0 copy-done.2
  141.9 2.2 %multiply_subtract_fusion.2 = (f32[96,3,192]{2,0,1:T(8,128)}, f32[96,3,192]{2,0,1:T(8,128)}, f32[96,3,192]{2,0,1:T(8,128)}) fusion(f32[96,3,192]{2,0,1:T(8,128)S(1)} %copy-done.2, f32[3,96,192]{2,1,0:T(8,128)} %get-tuple-element.28, f32[]{:T(128)S(6)} %min.3, f32[96,3,192]{2,0,1:T(8,128)} %param.28, f32[96,3,192]{2,0,1:T(8,128)} %param.33), kind=kLoop, calls=%fused_computation.17 | loop fusion | flops 884736 | bytes 1548292 | tf_op jit(solution)/shard_map/sub | solution.py:41
  144.1 0.0 copy-done.6
  144.1 0.0 copy-done.11
  144.1 0.0 copy-done.12
  144.1 0.0 copy-done.13
  144.1 0.8 multiply_subtract_fusion.3
  144.9 0.0 copy-done.5
  144.9 0.0 copy-done.7
  144.9 0.0 copy-done.8
  144.9 0.0 copy-start.14
  144.9 1.1 multiply_subtract_fusion.1
  145.9 0.0 copy-done.9
  145.9 0.0 copy-done.10
  146.0 1.1 multiply_subtract_fusion
  147.0 0.0 copy-done.14
  147.0 0.0 copy-done.16
  147.0 0.0 copy-done.17
  147.0 0.7 multiply_subtract_fusion.4
  147.7 0.0 copy-done.1
  147.7 1.1 copy.42
  148.9 1.3 copy-done
  150.2 1.7 %copy.43 = f32[2,512,768]{2,1,0:T(8,128)} copy(f32[2,512,768]{2,1,0:T(8,128)S(1)} %copy-done) | data formatting | bytes 6291456
  (20 shorter events, 0.1 us)
Async XLA Ops:
  0.7 7.3 %copy-start.4 = (f32[768,96]{0,1:T(8,128)S(1)}, f32[768,96]{0,1:T(8,128)}, u32[]{:S(2)}) copy-start(f32[768,96]{0,1:T(8,128)} %param.26) | copy-start | bytes 884740
  0.7 7.4 %copy-start.3 = (f32[96,768]{1,0:T(8,128)S(1)}, f32[96,768]{1,0:T(8,128)}, u32[]{:S(2)}) copy-start(f32[96,768]{1,0:T(8,128)} %param.25) | copy-start | bytes 884740
  3.9 4.9 %copy-start.15 = (f32[4,96]{1,0:T(4,128)S(1)}, f32[4,96]{1,0:T(4,128)}, u32[]{:S(2)}) copy-start(f32[4,96]{1,0:T(4,128)} %param.27) | copy-start | bytes 4612
  9.4 132.5 %copy-start.2 = (f32[96,3,192]{2,0,1:T(8,128)S(1)}, f32[96,3,192]{2,0,1:T(8,128)}, u32[]{:S(2)}) copy-start(f32[96,3,192]{2,0,1:T(8,128)} %param.23) | copy-start | bytes 663556
  139.8 4.3 %copy-start.6 = (f32[192,96]{1,0:T(8,128)S(1)}, f32[192,96]{1,0:T(8,128)}, u32[]{:S(2)}) copy-start(f32[192,96]{1,0:T(8,128)} %param.24) | copy-start | bytes 221188
  139.8 4.3 %copy-start.11 = (f32[192,96]{1,0:T(8,128)S(1)}, f32[192,96]{1,0:T(8,128)}, u32[]{:S(2)}) copy-start(f32[192,96]{1,0:T(8,128)} %param.29) | copy-start | bytes 221188
  139.8 4.3 %copy-start.12 = (f32[192,96]{1,0:T(8,128)S(1)}, f32[192,96]{1,0:T(8,128)}, u32[]{:S(2)}) copy-start(f32[192,96]{1,0:T(8,128)} %param.34) | copy-start | bytes 221188
  139.8 4.3 %copy-start.13 = (f32[192,96]{1,0:T(8,128)S(1)}, f32[192,96]{1,0:T(8,128)}, u32[]{:S(2)}) copy-start(f32[192,96]{1,0:T(8,128)} %get-tuple-element.29) | copy-start | bytes 221188
  139.8 5.0 %copy-start.5 = (f32[2,96,768]{2,1,0:T(8,128)S(1)}, f32[2,96,768]{2,1,0:T(8,128)}, u32[]{:S(2)}) copy-start(f32[2,96,768]{2,1,0:T(8,128)} %get-tuple-element.30) | copy-start | bytes 1769476
  139.8 5.0 %copy-start.7 = (f32[96,768]{1,0:T(8,128)S(1)}, f32[96,768]{1,0:T(8,128)}, u32[]{:S(2)}) copy-start(f32[96,768]{1,0:T(8,128)} %param.30) | copy-start | bytes 884740
  139.9 5.0 %copy-start.8 = (f32[96,768]{1,0:T(8,128)S(1)}, f32[96,768]{1,0:T(8,128)}, u32[]{:S(2)}) copy-start(f32[96,768]{1,0:T(8,128)} %param.35) | copy-start | bytes 884740
  144.1 1.9 %copy-start.9 = (f32[768,96]{0,1:T(8,128)S(1)}, f32[768,96]{0,1:T(8,128)}, u32[]{:S(2)}) copy-start(f32[768,96]{0,1:T(8,128)} %param.31) | copy-start | bytes 884740
  144.1 1.9 %copy-start.10 = (f32[768,96]{0,1:T(8,128)S(1)}, f32[768,96]{0,1:T(8,128)}, u32[]{:S(2)}) copy-start(f32[768,96]{0,1:T(8,128)} %param.36) | copy-start | bytes 884740
  144.9 2.1 %copy-start.14 = (f32[2,2,768]{2,1,0:T(2,128)S(1)}, f32[2,2,768]{2,1,0:T(2,128)}, u32[]{:S(2)}) copy-start(f32[2,2,768]{2,1,0:T(2,128)} %get-tuple-element.31) | copy-start | bytes 36868
  145.9 1.1 copy-start.16
  145.9 1.1 copy-start.17
  145.9 1.8 %copy-start.1 = (bf16[2,512,768]{2,1,0:T(8,128)(2,1)S(1)}, bf16[2,512,768]{2,1,0:T(8,128)(2,1)}, u32[]{:S(2)}) copy-start(bf16[2,512,768]{2,1,0:T(8,128)(2,1)} %get-tuple-element.84) | copy-start | bytes 4718596
  147.7 2.5 %copy-start = (f32[2,512,768]{2,1,0:T(8,128)S(1)}, f32[2,512,768]{2,1,0:T(8,128)}, u32[]{:S(2)}) copy-start(f32[2,512,768]{2,1,0:T(8,128)} %get-tuple-element.85) | copy-start | bytes 9437188

commit v3 on v2

--- a/solution.py
+++ b/solution.py
@@ -63,15 +63,16 @@
 
 def layer_kernel(
     dims,
-    x_ref, cot_ref, emb_ref, lc_ref, lr_ref, ain_ref, bin_ref, npin_ref,
+    x_in, cot_in, ids_ref, step_ref, wqkv_ref, wout_ref, wup_ref, wdown_ref, wnorm_ref,
     bo_ref, ig_ref, ga_ref, go_ref, gb_ref, gn_ref, gs_ref,
+    x_ref, cot_ref, emb, lc, npin,
     wag, wqkv, woall, wo4, wb, npg, npt,
     normed, qkv, probs, ctx, ctxp, ctxr, n2, hid, dpre, mid, dmid, bo_own, dattn, dqkv,
-    csend, crecv, own, ysend, yrecv,
+    csend, crecv, own, ysend, yrecv, bsend, brecv, bown, bysend, byrecv,
     gfo, gfb, rax_s, rax_r, raz_s, raz_r, rbx_s, rbx_r, rbz_s, rbz_r,
     nacc, ncore, nsum, sqd, sqt,
     az_s, az_r, ax_s, ax_r, np_s, np_r, oy_s, oy_r, oc_s, oc_r, cx_s, cx_r,
-    c_s, c_r, y_s, y_r, g_s, g_r, o_l,
+    c_s, c_r, y_s, y_r, g_s, g_r, o_l, in_l,
     rx_s, rx_r, rz_s, rz_r, nc_s, nc_r, nd_s, nd_r, qd_s, qd_r, qt_s, qt_r,
 ):
     micro, tok, width, n_dp, n_tp, heads = dims
@@ -94,6 +95,9 @@
 
     far = lax.div(z, 2)
     column = (z + 1 - 2 * lax.rem(z, 2), 2 - far, 3 - 3 * far)
+    inner = (z > 0) & (z < n_z - 1)
+    near_peer = (2 * column[0] + xx, tp)
+    mid_peer = (2 * column[1] + xx, tp)
     flip = 1 - xx
 
     def dp_of(k):
@@ -102,7 +106,7 @@
     def tp_of(k):
         return lax.rem(tp + k, n_tp)
 
-    sent = []
+    sent, sent_inner = [], []
 
     def copy(src, dst, s_sem, r_sem, peer):
         return pltpu.make_async_remote_copy(
@@ -114,8 +118,37 @@
         item.start()
         sent.append(item)
 
+    def send_inner(src, dst, s_sem, r_sem, peer):
+        item = copy(src, dst, s_sem, r_sem, peer)
+        pl.when(inner)(item.start)
+        sent_inner.append(item)
+
     def arrive(dst, s_sem, r_sem, peer):
         copy(dst, dst, s_sem, r_sem, peer).wait_recv()
+
+    loads = [
+        pltpu.make_async_copy(x_in, x_ref, in_l.at[0]),
+        pltpu.make_async_copy(cot_in, cot_ref, in_l.at[1]),
+    ]
+    for load in loads:
+        load.start()
+    for i in range(3):
+        wag[dp, :, 128 * i : 128 * (i + 1)] = fold(wqkv_ref[i]).astype(BF)
+    wag[dp, :, 384:512] = fold(wout_ref[...].T).astype(BF)
+    wb[0, dp] = wup_ref[...].astype(BF)
+    wb[1, dp] = wdown_ref[...].astype(BF)
+    npin[...] = jnp.zeros_like(npin)
+    npin[:4, :own_rows] = wnorm_ref[...].astype(BF)
+    place = lax.broadcasted_iota(jnp.int32, (1, width // 2), 1).astype(F32)
+    rates = jnp.exp(place * (-math.log(10000.0) / (width // 2)))
+    for m in range(micro):
+        angles = step_ref[:, m : m + 1].astype(F32) * rates
+        emb[m : m + 1, : width // 2] = jnp.sin(angles)
+        emb[m : m + 1, width // 2 :] = jnp.cos(angles)
+    labels = ids_ref[...].astype(F32)
+    columns = jnp.concatenate([labels] * (8 // micro), axis=0).T
+    for m in range(micro):
+        lc[m] = columns[:, m : m + 1]
 
     barrier = pltpu.get_barrier_semaphore()
     for k in range(1, n_dp):
@@ -133,29 +166,25 @@
     mine = half_rows(cc)
     other = half_rows(1 - cc)
 
-    def ag_src(g):
-        if g < 2:
-            return ain_ref.at[:, pl.ds(384 * g, 384 - 256 * g)]
-        return bin_ref.at[g - 2]
-
     def ag_at(g, j):
         if g < 2:
             return wag.at[j, :, pl.ds(384 * g, 384 - 256 * g)]
         return wb.at[g - 2, j]
 
     def ag_column(g):
-        for i in range(3):
-            send(ag_src(g), ag_at(g, dp), az_s.at[g, i], az_r.at[g, z], (2 * column[i] + xx, tp))
-        ag_at(g, dp)[...] = ag_src(g)[...]
+        block = ag_at(g, dp)
+        send(block, block, az_s.at[g, 0], az_r.at[g, 0], near_peer)
+        send_inner(block, block, az_s.at[g, 1], az_r.at[g, 1], mid_peer)
 
     def ag_side(g):
-        send(ag_src(g), ag_at(g, dp), ax_s.at[g, 3], ax_r.at[g, z], x_peer)
+        send(ag_at(g, dp), ag_at(g, dp), ax_s.at[g, 3], ax_r.at[g, z], x_peer)
 
     def ag_pass(g, *which):
         for i in which:
             s = column[i]
             block = ag_at(g, 2 * s + xx)
-            arrive(block, az_s.at[g, i], az_r.at[g, s], (2 * s + xx, tp))
+            arrive(block, az_s.at[g, 0], az_r.at[g, i], near_peer)
+            send_inner(block, block, az_s.at[g, 2 + i], az_r.at[g, i or 2], near_peer if i else mid_peer)
             send(block, block, ax_s.at[g, i], ax_r.at[g, s], x_peer)
 
     def ag_done(g):
@@ -183,19 +212,27 @@
         for t in range(n_tp):
             wo4[t] = unfold(woall[t]).reshape(width, local)
 
+    def ar_refs(kind, m):
+        if kind < 2:
+            return csend.at[kind, m], crecv.at[kind, m], own.at[m], ysend.at[kind, m], yrecv.at[kind, m]
+        return [r.at[kind - 2, m] for r in (bsend, brecv, bown, bysend, byrecv)]
+
     def ar_start(kind, m, part):
-        csend[kind, m] = part(other).astype(BF)
-        send(csend.at[kind, m], crecv.at[kind, m], c_s.at[kind, m], c_r.at[kind, m], c_peer)
-        own[kind % 2, m] = part(mine)
+        here, there, keep, _, _ = ar_refs(kind, m)
+        here[...] = part(other).astype(BF)
+        send(here, there, c_s.at[kind, m], c_r.at[kind, m], c_peer)
+        keep[...] = part(mine)
 
     def ar_cross(kind, m):
-        arrive(crecv.at[kind, m], c_s.at[kind, m], c_r.at[kind, m], c_peer)
-        ysend[kind, m] = (own[kind % 2, m] + crecv[kind, m].astype(F32)).astype(BF)
-        send(ysend.at[kind, m], yrecv.at[kind, m], y_s.at[kind, m], y_r.at[kind, m], y_peer)
+        _, there, keep, here, across = ar_refs(kind, m)
+        arrive(there, c_s.at[kind, m], c_r.at[kind, m], c_peer)
+        here[...] = (keep[...] + there[...].astype(F32)).astype(BF)
+        send(here, across, y_s.at[kind, m], y_r.at[kind, m], y_peer)
 
     def ar_total(kind, m):
-        arrive(yrecv.at[kind, m], y_s.at[kind, m], y_r.at[kind, m], y_peer)
-        return ysend[kind, m].astype(F32) + yrecv[kind, m].astype(F32)
+        _, _, _, here, across = ar_refs(kind, m)
+        arrive(across, y_s.at[kind, m], y_r.at[kind, m], y_peer)
+        return here[...].astype(F32) + across[...].astype(F32)
 
     def share(i, m, ref):
         send(ref.at[m, mine], ref.at[m, mine], g_s.at[i, m], g_r.at[i, m], c_peer)
@@ -233,7 +270,7 @@
         return npt[pl.ds(i, 1), :]
 
     def stream_of(m, rows):
-        return x_ref[m, rows, :].astype(F32) + emb_ref[m]
+        return x_ref[m, rows, :].astype(F32) + emb[pl.ds(m, 1), :]
 
     def first_norm(m):
         c0, inv = centred(stream_of(m, pl.ds(0, tok)))
@@ -254,7 +291,7 @@
         return jnp.where(here, value, 0.0).astype(BF)
 
     def attend(m, *between):
-        same = lc_ref[m] == lr_ref[m]
+        same = lc[m] == ids_ref[pl.ds(m, 1), :].astype(F32)
         total = None
         for h in range(heads):
             s = mm(qkv[0, m] * head_mask(h, scale), qkv[1, m], 1, 1)
@@ -295,13 +332,24 @@
         cdf = 0.5 * (1.0 + lax.erf(pre * math.sqrt(0.5)))
         hid[m] = (pre * cdf).astype(BF)
         slope = cdf + pre * (jnp.exp(-0.5 * pre * pre) * (1.0 / math.sqrt(2.0 * math.pi)))
+        if m == 0:
+            gfb[0, :tok, :] = slope
+        else:
+            dmid[...] = slope.reshape(2, half, slope.shape[-1])
+
+    def feed_back(m):
+        slope = gfb[0, :tok, :] if m == 0 else dmid[...].reshape(tok, dmid.shape[-1])
         dpre[m] = (mm(cot_ref[m], wide(1), 1, 0) * slope).astype(BF)
 
     def dn2_part(m):
         return lambda rows: mm(dpre[m, rows, :], wide(0), 1, 1)
 
-    def branch_part(m):
-        return lambda rows: mm(hid[m, rows, :], wide(1), 1, 1)
+    def branch_part(m, col):
+        def part(rows):
+            blocks = [wb[1, 2 * at + col] for at in range(n_z)]
+            return mm(hid[m, rows, :], jnp.concatenate(blocks, axis=0), 1, 1)
+
+        return part
 
     def col_sum(v):
         return jnp.sum(v, axis=0, keepdims=True)
@@ -318,7 +366,14 @@
         share(1, m, dattn)
 
     def finish_block(m):
-        bo_own[m] = (mid[m] + ar_total(1, m)).astype(BF)
+        near, away = ar_total(2, m), ar_total(3, m)
+        even = jnp.where(xx == 0, near, away)
+        odd = jnp.where(xx == 0, away, near)
+        pieces = []
+        for at in range(n_z):
+            cut = slice(at * own_rows, (at + 1) * own_rows)
+            pieces += [even[:, cut], odd[:, cut]]
+        bo_own[m] = (mid[m] + jnp.concatenate(pieces, axis=1)).astype(BF)
         send(bo_own.at[m], bo_ref.at[m, mine], g_s.at[2, m], g_r.at[2, m], c_peer)
         pltpu.make_async_copy(bo_own.at[m], bo_ref.at[m, mine], o_l.at[0, m]).start()
 
@@ -356,7 +411,7 @@
         return part
 
     def first_back(m):
-        grad = ar_total(2, m)
+        grad = ar_total(1, m)
         c0, inv = centred(stream_of(m, mine))
         hat = c0 * inv
         nacc[m, pl.ds(2, 1), :] = col_sum(grad * hat)
@@ -369,7 +424,7 @@
         if g == 0:
             rows = pl.ds(pl.multiple_of(col * fold_rows, fold_rows), fold_rows)
             return probs.at[at, rows, pl.ds(0, 384)]
-        return gfo.at[2 * at + col] if g == 1 else gfb.at[g - 2, 2 * at + col]
+        return gfo.at[2 * at + col] if g == 1 else gfb.at[g - 2, rows_of(2 * at + col)]
 
     def rs_slots(g, at):
         if g < 2:
@@ -381,7 +436,7 @@
         return ref[...].reshape(micro * tok, ref.shape[-1])
 
     def rs_wide(g, left, right):
-        gfb[g - 2] = mm(flat(left), flat(right), 0, 0).reshape(n_dp, own_rows, right.shape[-1])
+        gfb[g - 2] = mm(flat(left), flat(right), 0, 0)
 
     def rs_narrow(i, left, right):
         grad = fold(mm(flat(left), flat(right), 0, 0).reshape(n_dp, own_rows, local))
@@ -448,81 +503,97 @@
         total = nsum[e, 0]
         for j in range(1, n_dp):
             total = total + nsum[e, j]
-        gn_ref[e] = total
+        mine_only = jnp.zeros((2, own_rows), F32)
+        for j in range(n_dp):
+            mine_only = jnp.where(dp == j, total[:, j * own_rows : (j + 1) * own_rows], mine_only)
+        gn_ref[pl.ds(2 - 2 * e, 2), :] = mine_only
         return jnp.sum(col_sum(total * total), axis=1, keepdims=True)
 
     ag_side(0)
     ag_column(0)
-    npg[dp] = npin_ref[...]
+    ag_column(1)
+    ag_side(1)
+    npg[dp] = npin[...]
     for k in range(1, n_dp):
-        send(npin_ref, npg.at[dp], np_s.at[k], np_r.at[k], (dp_of(k), tp))
-    ag_column(1)
+        send(npin, npg.at[dp], np_s.at[k], np_r.at[k], (dp_of(k), tp))
     o_send(xx, (3,))
+    ag_side(2)
+    ag_pass(0, 0)
     for k in range(1, n_dp):
         arrive(npg.at[lax.rem(dp + n_dp - k, n_dp)], np_s.at[k], np_r.at[k], (dp_of(k), tp))
     open_norms()
+    loads[0].wait()
+    ag_pass(0, 1)
     first_norm(0)
-    ag_pass(0, 0)
+    ag_pass(0, 2)
+    ag_pass(1, 0)
+    ag_column(2)
     first_norm(1)
-    ag_pass(0, 1, 2)
-    ag_side(1)
-    ag_column(2)
-    ag_pass(1, 0, 1, 2)
-    o_send(xx, (0, 1, 2))
+    ag_pass(1, 1, 2)
     ag_done(0)
     open_qkv()
     project(0)
-    ag_side(2)
+    ag_column(3)
+    o_send(xx, (0, 1, 2))
+    project(1)
+    ag_pass(2, 0)
 
     def o_rest():
         ag_done(1)
         o_send(flip, (0, 1, 2, 3))
         o_core()
 
-    attend(0, (o_rest,), (partial(ag_pass, 2, 0),), (partial(ag_pass, 2, 1), partial(ag_column, 3)))
-    project(1)
-    ag_pass(2, 2)
-    ag_side(3)
-    attend(1, (o_across,), (partial(ag_pass, 3, 0),), (partial(ag_pass, 3, 1),))
+    attend(0, (o_rest, partial(ag_pass, 2, 1)), (partial(ag_pass, 2, 2),), (partial(ag_side, 3),))
+    attend(1, (partial(ag_pass, 3, 0),), (partial(ag_pass, 3, 1),), (o_across,))
     o_done()
     second_norm(0)
+    second_norm(1)
+    ag_pass(3, 2)
     ag_done(2)
-    ag_pass(3, 2)
-    second_norm(1)
+    loads[1].wait()
+    feed(0)
+    ar_start(2, 0, branch_part(0, xx))
+    feed(1)
+    ar_cross(2, 0)
+    ar_start(2, 1, branch_part(1, xx))
+    rs_wide(3, cot_ref, hid)
+    ar_cross(2, 1)
     ag_done(3)
-    feed(0)
+    feed_back(0)
     ar_start(0, 0, dn2_part(0))
-    feed(1)
+    rs_start(3)
+    feed_back(1)
     ar_cross(0, 0)
     ar_start(0, 1, dn2_part(1))
-    rs_wide(3, cot_ref, hid)
+    rs_wide(2, n2, dpre)
     ar_cross(0, 1)
-    rs_start(3)
-    rs_wide(2, n2, dpre)
-    ar_start(1, 0, branch_part(0))
-    ar_start(1, 1, branch_part(1))
+    rs_start(2)
+    rs_pass(3, 2, 1)
     second_back(0)
-    rs_pass(3, 2, 1)
-    attend_back(0, (partial(rs_pass, 3, 0),), (partial(rs_start, 2),))
-    ar_start(2, 0, dn1_part(0))
+    rs_pass(3, 0)
+    attend_back(0)
+    ar_start(1, 0, dn1_part(0))
     rs_pass(2, 2)
-    ar_cross(2, 0)
+    ar_cross(1, 0)
     second_back(1)
     rs_pass(2, 1)
     norm_start(0)
     attend_back(
         1,
-        (partial(rs_pass, 2, 0), partial(rs_narrow, 3, dattn, ctx), partial(rs_start, 1)),
+        (partial(rs_narrow, 3, dattn, ctx), partial(rs_start, 1), partial(rs_pass, 2, 0)),
         (partial(norm_cross, 0),),
     )
-    ar_start(2, 1, dn1_part(1))
+    ar_start(1, 1, dn1_part(1))
+    rs_narrow(0, normed, dqkv.at[0])
+    ar_cross(1, 1)
+    rs_narrow(1, normed, dqkv.at[1])
+    rs_narrow(2, normed, dqkv.at[2])
+    rs_start(0)
     rs_pass(1, 2, 1, 0)
-    for i in range(3):
-        rs_narrow(i, normed, dqkv.at[i])
-    ar_cross(2, 1)
-    rs_start(0)
-    ar_cross(1, 0)
-    ar_cross(1, 1)
+    ar_start(3, 0, branch_part(0, flip))
+    ar_start(3, 1, branch_part(1, flip))
+    ar_cross(3, 0)
+    ar_cross(3, 1)
     first_back(0)
     rs_pass(0, 2, 1)
     squares = rs_finish(3) + rs_finish(2)
@@ -561,14 +632,16 @@
         pltpu.make_async_copy(dmid.at[m], ig_ref.at[m, mine], o_l.at[1, m]).wait()
     for item in sent:
         item.wait_send()
-
-
-def layer_call(n_dp, n_tp, inputs, cotangent, item_ids, embeds, a_in, b_in, np_in):
+    for item in sent_inner:
+        pl.when(inner)(item.wait_send)
+
+
+def layer_call(n_dp, n_tp, inputs, cotangent, item_ids, timestep, qkv, out, up, down, norms):
     micro, tok, width = inputs.shape
-    _, own_rows, ff = b_in.shape
-    fold_rows = a_in.shape[0]
-    heads = 2 * a_in.shape[0] * a_in.shape[1] // (8 * own_rows * HEAD_DIM)
-    local = heads * HEAD_DIM
+    own_rows, ff = up.shape
+    local = qkv.shape[2]
+    fold_rows = 3 * own_rows // 2
+    heads = local // HEAD_DIM
     half = tok // 2
     fold_half = 3 * half // 2
     dims = (micro, tok, width, n_dp, n_tp, heads)
@@ -577,6 +650,7 @@
     n_z = n_dp // 2
     room = max(micro * heads, n_z)
     scratch = [
+        V((micro, tok, width), BF), V((micro, tok, width), BF), V((micro, width), F32), V((micro, tok, 1), F32), V((8, 128), BF),
         V((n_dp, fold_rows, 512), BF), V((3, width, local), BF), V((n_tp, n_dp, fold_rows, 128), BF),
         V((n_tp, width, local), BF), V((2, n_dp, own_rows, ff), BF), V((n_dp, 8, 128), BF), V((8, width), F32),
         V((micro, tok, width), BF), V((3, micro, tok, local), BF), V((room, tok, tok), F32),
@@ -584,17 +658,19 @@
         V((micro, tok, width), BF), V((micro, tok, ff), BF), V((micro, tok, ff), BF),
         V((micro, half, width), F32), V((micro, half, width), F32), V((micro, half, width), BF),
         V((micro, tok, width), BF), V((3, micro, tok, local), BF),
-        V((3, micro, half, width), BF), V((3, micro, half, width), BF), V((2, micro, half, width), F32),
-        V((3, micro, half, width), BF), V((3, micro, half, width), BF),
-        V((n_dp, fold_rows, 128), F32), V((2, n_dp, own_rows, ff), F32),
+        V((2, micro, half, width), BF), V((2, micro, half, width), BF), V((micro, half, width), F32),
+        V((2, micro, half, width), BF), V((2, micro, half, width), BF),
+        V((2, micro, half, width // 2), BF), V((2, micro, half, width // 2), BF), V((2, micro, half, width // 2), F32),
+        V((2, micro, half, width // 2), BF), V((2, micro, half, width // 2), BF),
+        V((n_dp, fold_rows, 128), F32), V((2, width, ff), F32),
         V((n_z, fold_rows, 512), BF), V((n_z, fold_rows, 512), BF), V((n_z, fold_rows, 512), BF), V((n_z, fold_rows, 512), BF),
         V((2, n_z, own_rows, ff), BF), V((2, n_z, own_rows, ff), BF), V((2, n_z, own_rows, ff), BF), V((2, n_z, own_rows, ff), BF),
         V((micro, 8, width), F32), V((2, 2, 2, width), F32), V((2, n_dp, 2, width), F32),
         V((n_dp, 8, 128), F32), V((n_tp, 8, 128), F32),
-        DMA((4, n_z)), DMA((4, n_z)), DMA((4, n_z)), DMA((4, n_z)), DMA((n_dp,)), DMA((n_dp,)), DMA((n_dp,)), DMA((n_dp,)), DMA((2,)), DMA((2,)),
+        DMA((4, 5)), DMA((4, 3)), DMA((4, n_z)), DMA((4, n_z)), DMA((n_dp,)), DMA((n_dp,)), DMA((n_dp,)), DMA((n_dp,)), DMA((2,)), DMA((2,)),
         DMA((micro, 3)), DMA((micro, 3)),
-        DMA((3, micro)), DMA((3, micro)), DMA((3, micro)), DMA((3, micro)), DMA((4, micro)), DMA((4, micro)),
-        DMA((2, micro)),
+        DMA((4, micro)), DMA((4, micro)), DMA((4, micro)), DMA((4, micro)), DMA((4, micro)), DMA((4, micro)),
+        DMA((2, micro)), DMA((2,)),
         DMA((4, n_z)), DMA((4, n_z)), DMA((4, n_z)), DMA((4, n_z)), DMA((2,)), DMA((2,)), DMA((2, n_dp)), DMA((2, n_dp)),
         DMA((n_dp,)), DMA((n_dp,)), DMA((n_tp,)), DMA((n_tp,)),
     ]
@@ -606,19 +682,76 @@
         out_shape=(
             S((micro, tok, width), BF), S((micro, tok, width), F32),
             S((3, own_rows, local), F32), S((local, own_rows), F32), S((2, own_rows, ff), F32),
-            S((2, 2, width), F32), S((8, 128), F32),
+            S((4, own_rows), F32), S((8, 128), F32),
         ),
-        in_specs=[vm] * 8,
+        in_specs=[anywhere] * 2 + [vm] * 7,
         out_specs=(anywhere, anywhere, vm, vm, vm, vm, vm),
         scratch_shapes=scratch,
         compiler_params=pltpu.CompilerParams(
             collective_id=0, has_side_effects=True, vmem_limit_bytes=63 << 20
         ),
         name="layer",
-    )(
-        inputs, cotangent, embeds[:, None, :],
-        item_ids[:, :, None], item_ids[:, None, :], a_in, b_in, np_in,
-    )
+    )(inputs, cotangent, item_ids, timestep, qkv, out, up, down, norms)
+
+
+def adam_kernel(*refs):
+    bo_in, ig_in, gs_ref = refs[:3]
+    grads = (refs[3], refs[4], refs[5].at[0], refs[5].at[1], refs[6])
+    olds = refs[7:22]
+    bo_ref, ig_ref, norm_ref = refs[22:25]
+    news = refs[25:40]
+    loaded, stored = refs[40:55], refs[55:70]
+    bo_held, ig_held, in_sem, out_sem, move_sem = refs[70:]
+    takes = [
+        pltpu.make_async_copy(bo_in, bo_held, move_sem.at[0]), pltpu.make_async_copy(ig_in, ig_held, move_sem.at[1])
+    ]
+    moves = [
+        pltpu.make_async_copy(bo_held, bo_ref, move_sem.at[2]), pltpu.make_async_copy(ig_held, ig_ref, move_sem.at[3])
+    ]
+    loads = [pltpu.make_async_copy(olds[i], loaded[i], in_sem.at[i]) for i in range(15)]
+    stores = [pltpu.make_async_copy(stored[i], news[i], out_sem.at[i]) for i in range(15)]
+    for load in loads:
+        load.start()
+    for take in takes:
+        take.start()
+    grad_norm = gs_ref[pl.ds(0, 1), pl.ds(0, 1)]
+    norm_ref[...] = grad_norm
+    factor = jnp.minimum(1.0, clip_limit / (grad_norm + 1e-06))
+    for p in range(5):
+        for i in range(3):
+            loads[3 * p + i].wait()
+        weight, first, second = loaded[3 * p : 3 * p + 3]
+        results = adam_step(weight[...], grads[p][...] * factor, first[...], second[...])
+        for i in range(3):
+            stored[3 * p + i][...] = results[i]
+            stores[3 * p + i].start()
+        if p in (1, 3):
+            takes[p // 2].wait()
+            moves[p // 2].start()
+    for store in stores:
+        store.wait()
+    for move in moves:
+        move.wait()
+
+
+def adam_call(block_out, grad_input, gs, grads, olds):
+    vm = pl.BlockSpec(memory_space=pltpu.VMEM)
+    anywhere = pl.BlockSpec(memory_space=pl.ANY)
+    S = jax.ShapeDtypeStruct
+    like = [S(o.shape, o.dtype) for o in olds]
+    return pl.pallas_call(
+        adam_kernel,
+        out_shape=(
+            S(block_out.shape, block_out.dtype), S(grad_input.shape, grad_input.dtype), S((1, 1), F32), *like
+        ),
+        in_specs=[anywhere] * 2 + [vm] * 5 + [anywhere] * 15,
+        out_specs=(anywhere, anywhere, vm, *[anywhere] * 15),
+        scratch_shapes=[pltpu.VMEM(o.shape, o.dtype) for o in olds] * 2
+        + [pltpu.VMEM(block_out.shape, block_out.dtype), pltpu.VMEM(grad_input.shape, grad_input.dtype)]
+        + [pltpu.SemaphoreType.DMA((15,)), pltpu.SemaphoreType.DMA((15,)), pltpu.SemaphoreType.DMA((4,))],
+        compiler_params=pltpu.CompilerParams(vmem_limit_bytes=63 << 20),
+        name="adam",
+    )(block_out, grad_input, gs, *grads, *olds)
 
 
 def fast_local(
@@ -627,28 +760,21 @@
     qkv_first, out_first, up_first, down_first, norm_first,
     qkv_second, out_second, up_second, down_second, norm_second,
 ):
-    embeds = time_embed(timestep[:, 0], inputs.shape[2])
-    narrow = [qkv_weight[:, i] for i in range(3)] + [out_weight.T]
-    a_in = jnp.concatenate([fold(w.astype(BF)) for w in narrow], axis=1)
-    b_in = jnp.stack([up_weight.astype(BF), down_weight.T.astype(BF)])
-    np_in = jnp.pad(norm_params.astype(BF), ((0, 4), (0, 128 - norm_params.shape[1])))
+    def turned(qkv, out, up, down, norms):
+        return (jnp.moveaxis(qkv, 1, 0), out, up, down.T, norms)
+
+    weights = turned(qkv_weight, out_weight, up_weight, down_weight, norm_params)
+    firsts = turned(qkv_first, out_first, up_first, down_first, norm_first)
+    seconds = turned(qkv_second, out_second, up_second, down_second, norm_second)
     block_out, grad_input, ga, go, gb, gn, gs = layer_call(
-        n_dp, n_tp, inputs, cotangent, item_ids, embeds, a_in, b_in, np_in
-    )
-    grad_norm = gs[0, 0]
-    factor = jnp.minimum(1.0, clip_limit / (grad_norm + 1e-06))
-    own = norm_params.shape[1]
-    gnorm_rows = jnp.concatenate([gn[1], gn[0]], axis=0)
-    gnorm_own = lax.dynamic_slice_in_dim(gnorm_rows, lax.axis_index("dp") * own, own, axis=1)
-    grads = (jnp.moveaxis(ga, 0, 1), go, gb[0], gb[1].T, gnorm_own)
-    weights = (qkv_weight, out_weight, up_weight, down_weight, norm_params)
-    firsts = (qkv_first, out_first, up_first, down_first, norm_first)
-    seconds = (qkv_second, out_second, up_second, down_second, norm_second)
-    result = [
-        adam_step(weights[index], grads[index] * factor, firsts[index], seconds[index]) for index in range(5)
-    ]
-    flat = [item for triple in result for item in triple]
-    return (block_out, grad_input, grad_norm, *flat)
+        n_dp, n_tp, inputs, cotangent, item_ids, timestep.T, *weights
+    )
+    olds = [item for p in range(5) for item in (weights[p], firsts[p], seconds[p])]
+    block_out, grad_input, grad_norm, *news = adam_call(block_out, grad_input, gs, (ga, go, gb, gn), olds)
+    for i in range(3):
+        news[i] = jnp.moveaxis(news[i], 0, 1)
+        news[9 + i] = news[9 + i].T
+    return (block_out, grad_input, grad_norm[0, 0], *news)
 
 
 def layer_norm(values, gain_row, bias_row):

time: 152 us -> 122 us (0.80)
  local copies, waits for them, and re-layouts: 10.7 us -> 0 us
  other arithmetic: 9.11 us -> 0 us
  Pallas kernels: 130 us -> 121 us
    pallas_call x1, Pallas kernels: 130 us -> 113 us  [layer_call(): pl.pallas_call(partial(layer_kernel, dims), out_shape=(S((micro, tok, wid...]
    pallas_call x0 -> x1, Pallas kernels: none -> 8.34 us  [adam_call(): pl.pallas_call(adam_kernel, out_shape=(S(block_out.shape, block_out.dtype...]
    sub x5 -> x0, other arithmetic: 5.73 us -> none  [adam_step(): weight - learn_rate * (moment_one / (jnp.sqrt(moment_two) + adam_eps) + w...]
    unnamed x39 -> x0, local copies, waits for them, and re-layouts: 5.18 us -> none
    broadcast_in_dim x3 -> x0, local copies, waits for them, and re-layouts: 3.6 us -> none  [the longest x1 1.71 us: layer_call(): item_ids[:, :, None]]
    another operation x4 -> x0, other arithmetic: 1.75 us -> none
where the time goes in v3:
time: 122 us
  Pallas kernels  121 us (99%)
    pallas_call x1, Pallas kernels, layer_call(): pl.pallas_call(partial(layer_kernel, dims), out_shape=(S((micro, tok, wid...  113 us
    pallas_call x1, Pallas kernels, adam_call(): pl.pallas_call(adam_kernel, out_shape=(S(block_out.shape, block_out.dtype...  8.34 us

profile of v3, /device:TPU:0, one launch (start us, length us, event | category | flops | bytes accessed | tf_op | source)
XLA Modules:
  0.0 121.9 jit_solution(7601629151611546630)
XLA Ops:
  0.7 112.7 %layer.1 = (bf16[2,512,768]{2,1,0:T(8,128)(2,1)}, f32[2,512,768]{2,1,0:T(8,128)}, f32[3,96,192]{2,1,0:T(8,128)}, f32[192,96]{1,0:T(8,128)}, f32[2,96,768]{2,1,0:...) custom-call(bf16[2,512,768]{2,1,0:T(8,128)(2,1)} %x_in.1, bf16[2,512,768]{2,1,0:T(8,128)(2,1)} %cot_in.1, s32[2,512]{1,0:T(2,128)} %ids_ref.1, ...), custom_call_target="tpu_custom_call" | custom-call | tf_op jit(solution)/shard_map/layer/pallas_call | solution.py:680
  113.4 8.3 %adam.1 = (bf16[2,512,768]{2,1,0:T(8,128)(2,1)}, f32[2,512,768]{2,1,0:T(8,128)}, f32[1,1]{1,0:T(1,128)}, f32[3,96,192]{2,1,0:T(8,128)}, f32[3,96,192]{2,1,0:T(8,...) custom-call(bf16[2,512,768]{2,1,0:T(8,128)(2,1)} %get-tuple-element., ...), custom_call_target="tpu_custom_call" | custom-call | tf_op jit(solution)/shard_map/adam/pallas_call | solution.py:742

commit v4 on v3

--- a/solution.py
+++ b/solution.py
@@ -65,11 +65,11 @@
     dims,
     x_in, cot_in, ids_ref, step_ref, wqkv_ref, wout_ref, wup_ref, wdown_ref, wnorm_ref,
     bo_ref, ig_ref, ga_ref, go_ref, gb_ref, gn_ref, gs_ref,
-    x_ref, cot_ref, emb, lc, npin,
+    x_ref, cot_ref, emb, lc, npin, ga, go, gb, gn, gs,
     wag, wqkv, woall, wo4, wb, npg, npt,
     normed, qkv, probs, ctx, ctxp, ctxr, n2, hid, dpre, mid, dmid, bo_own, dattn, dqkv,
     csend, crecv, own, ysend, yrecv, bsend, brecv, bown, bysend, byrecv,
-    gfo, gfb, rax_s, rax_r, raz_s, raz_r, rbx_s, rbx_r, rbz_s, rbz_r,
+    gfa, gfo, gfb, rax_s, rax_r, raz_s, raz_r, rbx_s, rbx_r, rbz_s, rbz_r,
     nacc, ncore, nsum, sqd, sqt,
     az_s, az_r, ax_s, ax_r, np_s, np_r, oy_s, oy_r, oc_s, oc_r, cx_s, cx_r,
     c_s, c_r, y_s, y_r, g_s, g_r, o_l, in_l,
@@ -106,7 +106,12 @@
     def tp_of(k):
         return lax.rem(tp + k, n_tp)
 
-    sent, sent_inner = [], []
+    sent, sent_inner, puts = [], [], []
+
+    def put(i, held, there):
+        item = pltpu.make_async_copy(held, there, in_l.at[2 + i])
+        item.start()
+        puts.append(item)
 
     def copy(src, dst, s_sem, r_sem, peer):
         return pltpu.make_async_remote_copy(
@@ -126,6 +131,11 @@
     def arrive(dst, s_sem, r_sem, peer):
         copy(dst, dst, s_sem, r_sem, peer).wait_recv()
 
+    barrier = pltpu.get_barrier_semaphore()
+    for k in range(1, n_dp):
+        pl.semaphore_signal(barrier, inc=1, device_id=(dp_of(k), tp), device_id_type=MESH)
+    for k in range(1, n_tp):
+        pl.semaphore_signal(barrier, inc=1, device_id=(dp, tp_of(k)), device_id_type=MESH)
     loads = [
         pltpu.make_async_copy(x_in, x_ref, in_l.at[0]),
         pltpu.make_async_copy(cot_in, cot_ref, in_l.at[1]),
@@ -150,11 +160,6 @@
     for m in range(micro):
         lc[m] = columns[:, m : m + 1]
 
-    barrier = pltpu.get_barrier_semaphore()
-    for k in range(1, n_dp):
-        pl.semaphore_signal(barrier, inc=1, device_id=(dp_of(k), tp), device_id_type=MESH)
-    for k in range(1, n_tp):
-        pl.semaphore_signal(barrier, inc=1, device_id=(dp, tp_of(k)), device_id_type=MESH)
     pl.semaphore_wait(barrier, n_dp + n_tp - 2)
 
     def rows_of(j):
@@ -187,8 +192,9 @@
             send_inner(block, block, az_s.at[g, 2 + i], az_r.at[g, i or 2], near_peer if i else mid_peer)
             send(block, block, ax_s.at[g, i], ax_r.at[g, s], x_peer)
 
-    def ag_done(g):
-        for i, s in enumerate((*column, z)):
+    def ag_done(g, *which):
+        for i in which or range(4):
+            s = (*column, z)[i]
             arrive(ag_at(g, 2 * s + flip), ax_s.at[g, i], ax_r.at[g, s], x_peer)
 
     def o_send(col, which):
@@ -337,17 +343,20 @@
         else:
             dmid[...] = slope.reshape(2, half, slope.shape[-1])
 
-    def feed_back(m):
-        slope = gfb[0, :tok, :] if m == 0 else dmid[...].reshape(tok, dmid.shape[-1])
-        dpre[m] = (mm(cot_ref[m], wide(1), 1, 0) * slope).astype(BF)
-
     def dn2_part(m):
-        return lambda rows: mm(dpre[m, rows, :], wide(0), 1, 1)
-
-    def branch_part(m, col):
         def part(rows):
-            blocks = [wb[1, 2 * at + col] for at in range(n_z)]
-            return mm(hid[m, rows, :], jnp.concatenate(blocks, axis=0), 1, 1)
+            at = 1 - cc if rows is other else cc
+            slope = gfb[0, rows, :] if m == 0 else dmid[at]
+            grad = (mm(cot_ref[m, rows, :], wide(1), 1, 0) * slope).astype(BF)
+            dpre[m, rows, :] = grad
+            return mm(grad, wide(0), 1, 1)
+
+        return part
+
+    def branch_part(m, side):
+        def part(rows):
+            blocks = wb[1, pl.ds(side * n_z, n_z)]
+            return mm(hid[m, rows, :], blocks.reshape(width // 2, blocks.shape[-1]), 1, 1)
 
         return part
 
@@ -367,13 +376,9 @@
 
     def finish_block(m):
         near, away = ar_total(2, m), ar_total(3, m)
-        even = jnp.where(xx == 0, near, away)
-        odd = jnp.where(xx == 0, away, near)
-        pieces = []
-        for at in range(n_z):
-            cut = slice(at * own_rows, (at + 1) * own_rows)
-            pieces += [even[:, cut], odd[:, cut]]
-        bo_own[m] = (mid[m] + jnp.concatenate(pieces, axis=1)).astype(BF)
+        left = jnp.where(far == 0, near, away)
+        right = jnp.where(far == 0, away, near)
+        bo_own[m] = (mid[m] + jnp.concatenate([left, right], axis=1)).astype(BF)
         send(bo_own.at[m], bo_ref.at[m, mine], g_s.at[2, m], g_r.at[2, m], c_peer)
         pltpu.make_async_copy(bo_own.at[m], bo_ref.at[m, mine], o_l.at[0, m]).start()
 
@@ -422,8 +427,7 @@
 
     def gf(g, at, col):
         if g == 0:
-            rows = pl.ds(pl.multiple_of(col * fold_rows, fold_rows), fold_rows)
-            return probs.at[at, rows, pl.ds(0, 384)]
+            return gfa.at[2 * at + col]
         return gfo.at[2 * at + col] if g == 1 else gfb.at[g - 2, rows_of(2 * at + col)]
 
     def rs_slots(g, at):
@@ -438,14 +442,17 @@
     def rs_wide(g, left, right):
         gfb[g - 2] = mm(flat(left), flat(right), 0, 0)
 
-    def rs_narrow(i, left, right):
-        grad = fold(mm(flat(left), flat(right), 0, 0).reshape(n_dp, own_rows, local))
-        if i == 3:
-            gfo[...] = grad
-            return
-        for j in range(n_dp):
-            rows = pl.ds((j % 2) * fold_rows, fold_rows)
-            probs[j // 2, rows, 128 * i : 128 * (i + 1)] = grad[j]
+    def folded(left, right):
+        return fold(mm(left, right, 0, 0).reshape(n_dp, own_rows, local))
+
+    def rs_out():
+        gfo[...] = folded(flat(dattn), flat(ctx))
+
+    def rs_qkv(m):
+        for i in range(3):
+            lanes = slice(128 * i, 128 * (i + 1))
+            grad = folded(normed[m], dqkv[i, m])
+            gfa[:, :, lanes] = grad if m == 0 else gfa[:, :, lanes] + grad
 
     def rs_start(g):
         for i in (2, 1, 0, 3):
@@ -476,11 +483,14 @@
             total = total + there[...].astype(F32)
         if g == 0:
             for i in range(3):
-                ga_ref[i] = unfold(total[:, 128 * i : 128 * (i + 1)])
+                ga[i] = unfold(total[:, 128 * i : 128 * (i + 1)])
+            put(0, ga, ga_ref)
         elif g == 1:
-            go_ref[...] = unfold(total).T
+            go[...] = unfold(total).T
+            put(1, go, go_ref)
         else:
-            gb_ref[g - 2] = total
+            gb[g - 2] = total
+            put(g, gb.at[g - 2], gb_ref.at[g - 2])
         return jnp.sum(col_sum(total * total), axis=1, keepdims=True)
 
     def norm_start(e):
@@ -506,7 +516,7 @@
         mine_only = jnp.zeros((2, own_rows), F32)
         for j in range(n_dp):
             mine_only = jnp.where(dp == j, total[:, j * own_rows : (j + 1) * own_rows], mine_only)
-        gn_ref[pl.ds(2 - 2 * e, 2), :] = mine_only
+        gn[pl.ds(2 - 2 * e, 2), :] = mine_only
         return jnp.sum(col_sum(total * total), axis=1, keepdims=True)
 
     ag_side(0)
@@ -517,7 +527,6 @@
     for k in range(1, n_dp):
         send(npin, npg.at[dp], np_s.at[k], np_r.at[k], (dp_of(k), tp))
     o_send(xx, (3,))
-    ag_side(2)
     ag_pass(0, 0)
     for k in range(1, n_dp):
         arrive(npg.at[lax.rem(dp + n_dp - k, n_dp)], np_s.at[k], np_r.at[k], (dp_of(k), tp))
@@ -528,6 +537,7 @@
     ag_pass(0, 2)
     ag_pass(1, 0)
     ag_column(2)
+    ag_side(2)
     first_norm(1)
     ag_pass(1, 1, 2)
     ag_done(0)
@@ -543,26 +553,30 @@
         o_send(flip, (0, 1, 2, 3))
         o_core()
 
-    attend(0, (o_rest, partial(ag_pass, 2, 1)), (partial(ag_pass, 2, 2),), (partial(ag_side, 3),))
-    attend(1, (partial(ag_pass, 3, 0),), (partial(ag_pass, 3, 1),), (o_across,))
+    attend(0, (o_rest,))
+    ag_pass(2, 1, 2)
+    ag_side(3)
+    ag_pass(3, 0)
+    attend(1)
+    ag_pass(3, 1)
+    o_across()
     o_done()
     second_norm(0)
     second_norm(1)
+    ag_done(2)
+    feed(0)
+    ag_done(3, 0, 3)
+    ar_start(2, 0, branch_part(0, far))
     ag_pass(3, 2)
-    ag_done(2)
-    loads[1].wait()
-    feed(0)
-    ar_start(2, 0, branch_part(0, xx))
     feed(1)
     ar_cross(2, 0)
-    ar_start(2, 1, branch_part(1, xx))
+    ar_start(2, 1, branch_part(1, far))
+    loads[1].wait()
     rs_wide(3, cot_ref, hid)
     ar_cross(2, 1)
-    ag_done(3)
-    feed_back(0)
+    ag_done(3, 1, 2)
     ar_start(0, 0, dn2_part(0))
     rs_start(3)
-    feed_back(1)
     ar_cross(0, 0)
     ar_start(0, 1, dn2_part(1))
     rs_wide(2, n2, dpre)
@@ -575,23 +589,18 @@
     ar_start(1, 0, dn1_part(0))
     rs_pass(2, 2)
     ar_cross(1, 0)
+    rs_qkv(0)
     second_back(1)
     rs_pass(2, 1)
     norm_start(0)
-    attend_back(
-        1,
-        (partial(rs_narrow, 3, dattn, ctx), partial(rs_start, 1), partial(rs_pass, 2, 0)),
-        (partial(norm_cross, 0),),
-    )
+    attend_back(1, (rs_out, partial(rs_start, 1), partial(rs_pass, 2, 0)), (partial(norm_cross, 0),))
+    rs_qkv(1)
+    rs_start(0)
     ar_start(1, 1, dn1_part(1))
-    rs_narrow(0, normed, dqkv.at[0])
+    rs_pass(1, 2, 1, 0)
     ar_cross(1, 1)
-    rs_narrow(1, normed, dqkv.at[1])
-    rs_narrow(2, normed, dqkv.at[2])
-    rs_start(0)
-    rs_pass(1, 2, 1, 0)
-    ar_start(3, 0, branch_part(0, flip))
-    ar_start(3, 1, branch_part(1, flip))
+    ar_start(3, 0, branch_part(0, 1 - far))
+    ar_start(3, 1, branch_part(1, 1 - far))
     ar_cross(3, 0)
     ar_cross(3, 1)
     first_back(0)
@@ -606,6 +615,7 @@
     sqd[dp] = jnp.broadcast_to(squares, (8, 128))
     for k in range(1, n_dp):
         send(sqd.at[dp], sqd.at[dp], qd_s.at[k], qd_r.at[k], (dp_of(k), tp))
+    finish_block(0)
     extra = norm_finish(0) + norm_finish(1)
     for k in range(1, n_dp):
         j = lax.rem(dp + n_dp - k, n_dp)
@@ -616,20 +626,23 @@
     sqt[tp] = mesh_row
     for k in range(1, n_tp):
         send(sqt.at[tp], sqt.at[tp], qt_s.at[k], qt_r.at[k], (dp, tp_of(k)))
+    finish_block(1)
     for k in range(1, n_tp):
         j = lax.rem(tp + n_tp - k, n_tp)
         arrive(sqt.at[j], qt_s.at[k], qt_r.at[k], (dp, tp_of(k)))
     everything = sqt[0]
     for j in range(1, n_tp):
         everything = everything + sqt[j]
-    gs_ref[...] = jnp.sqrt(everything + extra)
-    finish_block(0)
-    finish_block(1)
+    gs[...] = jnp.sqrt(everything + extra)
+    put(4, gn, gn_ref)
+    put(5, gs, gs_ref)
     for m in range(micro):
         arrive(bo_ref.at[m, other], g_s.at[2, m], g_r.at[2, m], c_peer)
         arrive(ig_ref.at[m, other], g_s.at[3, m], g_r.at[3, m], c_peer)
         pltpu.make_async_copy(bo_own.at[m], bo_ref.at[m, mine], o_l.at[0, m]).wait()
         pltpu.make_async_copy(dmid.at[m], ig_ref.at[m, mine], o_l.at[1, m]).wait()
+    for item in puts:
+        item.wait()
     for item in sent:
         item.wait_send()
     for item in sent_inner:
@@ -648,12 +661,12 @@
     V = pltpu.VMEM
     DMA = pltpu.SemaphoreType.DMA
     n_z = n_dp // 2
-    room = max(micro * heads, n_z)
     scratch = [
         V((micro, tok, width), BF), V((micro, tok, width), BF), V((micro, width), F32), V((micro, tok, 1), F32), V((8, 128), BF),
+        V((3, own_rows, local), F32), V((local, own_rows), F32), V((2, own_rows, ff), F32), V((4, own_rows), F32), V((8, 128), F32),
         V((n_dp, fold_rows, 512), BF), V((3, width, local), BF), V((n_tp, n_dp, fold_rows, 128), BF),
         V((n_tp, width, local), BF), V((2, n_dp, own_rows, ff), BF), V((n_dp, 8, 128), BF), V((8, width), F32),
-        V((micro, tok, width), BF), V((3, micro, tok, local), BF), V((room, tok, tok), F32),
+        V((micro, tok, width), BF), V((3, micro, tok, local), BF), V((micro * heads, tok, tok), F32),
         V((micro, tok, local), BF), V((micro, 2, fold_half, 128), BF), V((micro, n_tp, fold_half, 128), BF),
         V((micro, tok, width), BF), V((micro, tok, ff), BF), V((micro, tok, ff), BF),
         V((micro, half, width), F32), V((micro, half, width), F32), V((micro, half, width), BF),
@@ -662,7 +675,7 @@
         V((2, micro, half, width), BF), V((2, micro, half, width), BF),
         V((2, micro, half, width // 2), BF), V((2, micro, half, width // 2), BF), V((2, micro, half, width // 2), F32),
         V((2, micro, half, width // 2), BF), V((2, micro, half, width // 2), BF),
-        V((n_dp, fold_rows, 128), F32), V((2, width, ff), F32),
+        V((n_dp, fold_rows, 384), F32), V((n_dp, fold_rows, 128), F32), V((2, width, ff), F32),
         V((n_z, fold_rows, 512), BF), V((n_z, fold_rows, 512), BF), V((n_z, fold_rows, 512), BF), V((n_z, fold_rows, 512), BF),
         V((2, n_z, own_rows, ff), BF), V((2, n_z, own_rows, ff), BF), V((2, n_z, own_rows, ff), BF), V((2, n_z, own_rows, ff), BF),
         V((micro, 8, width), F32), V((2, 2, 2, width), F32), V((2, n_dp, 2, width), F32),
@@ -670,7 +683,7 @@
         DMA((4, 5)), DMA((4, 3)), DMA((4, n_z)), DMA((4, n_z)), DMA((n_dp,)), DMA((n_dp,)), DMA((n_dp,)), DMA((n_dp,)), DMA((2,)), DMA((2,)),
         DMA((micro, 3)), DMA((micro, 3)),
         DMA((4, micro)), DMA((4, micro)), DMA((4, micro)), DMA((4, micro)), DMA((4, micro)), DMA((4, micro)),
-        DMA((2, micro)), DMA((2,)),
+        DMA((2, micro)), DMA((8,)),
         DMA((4, n_z)), DMA((4, n_z)), DMA((4, n_z)), DMA((4, n_z)), DMA((2,)), DMA((2,)), DMA((2, n_dp)), DMA((2, n_dp)),
         DMA((n_dp,)), DMA((n_dp,)), DMA((n_tp,)), DMA((n_tp,)),
     ]
@@ -685,7 +698,7 @@
             S((4, own_rows), F32), S((8, 128), F32),
         ),
         in_specs=[anywhere] * 2 + [vm] * 7,
-        out_specs=(anywhere, anywhere, vm, vm, vm, vm, vm),
+        out_specs=[anywhere] * 7,
         scratch_shapes=scratch,
         compiler_params=pltpu.CompilerParams(
             collective_id=0, has_side_effects=True, vmem_limit_bytes=63 << 20
@@ -696,28 +709,33 @@
 
 def adam_kernel(*refs):
     bo_in, ig_in, gs_ref = refs[:3]
-    grads = (refs[3], refs[4], refs[5].at[0], refs[5].at[1], refs[6])
     olds = refs[7:22]
     bo_ref, ig_ref, norm_ref = refs[22:25]
     news = refs[25:40]
     loaded, stored = refs[40:55], refs[55:70]
-    bo_held, ig_held, in_sem, out_sem, move_sem = refs[70:]
-    takes = [
-        pltpu.make_async_copy(bo_in, bo_held, move_sem.at[0]), pltpu.make_async_copy(ig_in, ig_held, move_sem.at[1])
-    ]
-    moves = [
-        pltpu.make_async_copy(bo_held, bo_ref, move_sem.at[2]), pltpu.make_async_copy(ig_held, ig_ref, move_sem.at[3])
-    ]
+    bo_held, ig_held, ga, go, gb, gn, in_sem, out_sem, move_sem, grad_sem = refs[70:]
+    grads = (ga, go, gb.at[0], gb.at[1], gn)
+    held_grads = (ga, go, gb, gn)
+    gets = [pltpu.make_async_copy(refs[3 + i], held_grads[i], grad_sem.at[i]) for i in range(4)]
+    got = (0, 1, 2, None, 3)
+    takes, moves = [], []
+    for n, (there, held, here) in enumerate(((ig_in, ig_held, ig_ref), (bo_in, bo_held, bo_ref))):
+        takes.append(pltpu.make_async_copy(there, held, move_sem.at[0, n]))
+        moves.append(pltpu.make_async_copy(held, here, move_sem.at[1, n]))
     loads = [pltpu.make_async_copy(olds[i], loaded[i], in_sem.at[i]) for i in range(15)]
     stores = [pltpu.make_async_copy(stored[i], news[i], out_sem.at[i]) for i in range(15)]
-    for load in loads:
-        load.start()
+    for item in (gets[0], *loads[:3], *gets[1:]):
+        item.start()
     for take in takes:
         take.start()
+    for load in loads[3:]:
+        load.start()
     grad_norm = gs_ref[pl.ds(0, 1), pl.ds(0, 1)]
     norm_ref[...] = grad_norm
     factor = jnp.minimum(1.0, clip_limit / (grad_norm + 1e-06))
     for p in range(5):
+        if got[p] is not None:
+            gets[got[p]].wait()
         for i in range(3):
             loads[3 * p + i].wait()
         weight, first, second = loaded[3 * p : 3 * p + 3]
@@ -725,9 +743,10 @@
         for i in range(3):
             stored[3 * p + i][...] = results[i]
             stores[3 * p + i].start()
-        if p in (1, 3):
-            takes[p // 2].wait()
-            moves[p // 2].start()
+        if p == 0:
+            for take, move in zip(takes, moves):
+                take.wait()
+                move.start()
     for store in stores:
         store.wait()
     for move in moves:
@@ -744,11 +763,12 @@
         out_shape=(
             S(block_out.shape, block_out.dtype), S(grad_input.shape, grad_input.dtype), S((1, 1), F32), *like
         ),
-        in_specs=[anywhere] * 2 + [vm] * 5 + [anywhere] * 15,
+        in_specs=[anywhere] * 2 + [vm] + [anywhere] * 19,
         out_specs=(anywhere, anywhere, vm, *[anywhere] * 15),
         scratch_shapes=[pltpu.VMEM(o.shape, o.dtype) for o in olds] * 2
         + [pltpu.VMEM(block_out.shape, block_out.dtype), pltpu.VMEM(grad_input.shape, grad_input.dtype)]
-        + [pltpu.SemaphoreType.DMA((15,)), pltpu.SemaphoreType.DMA((15,)), pltpu.SemaphoreType.DMA((4,))],
+        + [pltpu.VMEM(g.shape, g.dtype) for g in grads]
+        + [pltpu.SemaphoreType.DMA((15,)), pltpu.SemaphoreType.DMA((15,)), pltpu.SemaphoreType.DMA((2, 2)), pltpu.SemaphoreType.DMA((4,))],
         compiler_params=pltpu.CompilerParams(vmem_limit_bytes=63 << 20),
         name="adam",
     )(block_out, grad_input, gs, *grads, *olds)

time: 122 us -> 117 us (0.959)
  Pallas kernels: 121 us -> 115 us
    pallas_call x1, Pallas kernels: 113 us -> 108 us  [layer_call(): pl.pallas_call(partial(layer_kernel, dims), out_shape=(S((micro, tok, wid...]
where the time goes in v4:
time: 117 us; the launch traced here: 116 us
  Pallas kernels  115 us (98%)
    pallas_call x1, Pallas kernels, layer_call(): pl.pallas_call(partial(layer_kernel, dims), out_shape=(S((micro, tok, wid...  108 us
    pallas_call x1, Pallas kernels, adam_call(): pl.pallas_call(adam_kernel, out_shape=(S(block_out.shape, block_out.dtype...  7.54 us

profile of v4, /device:TPU:0, one launch (start us, length us, event | category | flops | bytes accessed | tf_op | source)
XLA Modules:
  0.0 116.3 jit_solution(5827924689423033010)
XLA Ops:
  0.7 107.9 %layer.1 = (bf16[2,512,768]{2,1,0:T(8,128)(2,1)}, f32[2,512,768]{2,1,0:T(8,128)}, f32[3,96,192]{2,1,0:T(8,128)}, f32[192,96]{1,0:T(8,128)}, f32[2,96,768]{2,1,0:...) custom-call(bf16[2,512,768]{2,1,0:T(8,128)(2,1)} %x_in.1, bf16[2,512,768]{2,1,0:T(8,128)(2,1)} %cot_in.1, s32[2,512]{1,0:T(2,128)} %ids_ref.1, ...), custom_call_target="tpu_custom_call" | custom-call | tf_op jit(solution)/shard_map/layer/pallas_call | solution.py:693
  108.5 7.5 %adam.1 = (bf16[2,512,768]{2,1,0:T(8,128)(2,1)}, f32[2,512,768]{2,1,0:T(8,128)}, f32[1,1]{1,0:T(1,128)}, f32[3,96,192]{2,1,0:T(8,128)}, f32[3,96,192]{2,1,0:T(8,...) custom-call(bf16[2,512,768]{2,1,0:T(8,128)(2,1)} %get-tuple-element., ...), custom_call_target="tpu_custom_call" | custom-call | tf_op jit(solution)/shard_map/adam/pallas_call | solution.py:761

commit v5 on v4

--- a/solution.py
+++ b/solution.py
@@ -127,6 +127,14 @@
         item = copy(src, dst, s_sem, r_sem, peer)
         pl.when(inner)(item.start)
         sent_inner.append(item)
+
+    def settle(count):
+        for item in sent[:count]:
+            item.wait_send()
+        for item in sent_inner:
+            pl.when(inner)(item.wait_send)
+        del sent[:count]
+        sent_inner.clear()
 
     def arrive(dst, s_sem, r_sem, peer):
         copy(dst, dst, s_sem, r_sem, peer).wait_recv()
@@ -593,6 +601,7 @@
     second_back(1)
     rs_pass(2, 1)
     norm_start(0)
+    early = len(sent)
     attend_back(1, (rs_out, partial(rs_start, 1), partial(rs_pass, 2, 0)), (partial(norm_cross, 0),))
     rs_qkv(1)
     rs_start(0)
@@ -608,6 +617,7 @@
     squares = rs_finish(3) + rs_finish(2)
     squares = squares + rs_finish(1)
     rs_pass(0, 0)
+    settle(early)
     first_back(1)
     norm_start(1)
     norm_cross(1)
@@ -643,10 +653,7 @@
         pltpu.make_async_copy(dmid.at[m], ig_ref.at[m, mine], o_l.at[1, m]).wait()
     for item in puts:
         item.wait()
-    for item in sent:
-        item.wait_send()
-    for item in sent_inner:
-        pl.when(inner)(item.wait_send)
+    settle(len(sent))
 
 
 def layer_call(n_dp, n_tp, inputs, cotangent, item_ids, timestep, qkv, out, up, down, norms):

time: 117 us -> 116 us (level)
  no operation moved by 1% of the time
where the time goes in v5:
time: 116 us
  Pallas kernels  115 us (99%)
    pallas_call x1, Pallas kernels, layer_call(): pl.pallas_call(partial(layer_kernel, dims), out_shape=(S((micro, tok, wid...  108 us
    pallas_call x1, Pallas kernels, adam_call(): pl.pallas_call(adam_kernel, out_shape=(S(block_out.shape, block_out.dtype...  7.54 us

profile of v5, /device:TPU:0, one launch (start us, length us, event | category | flops | bytes accessed | tf_op | source)
XLA Modules:
  0.0 116.2 jit_solution(7474304240528623696)
XLA Ops:
  0.7 107.8 %layer.1 = (bf16[2,512,768]{2,1,0:T(8,128)(2,1)}, f32[2,512,768]{2,1,0:T(8,128)}, f32[3,96,192]{2,1,0:T(8,128)}, f32[192,96]{1,0:T(8,128)}, f32[2,96,768]{2,1,0:...) custom-call(bf16[2,512,768]{2,1,0:T(8,128)(2,1)} %x_in.1, bf16[2,512,768]{2,1,0:T(8,128)(2,1)} %cot_in.1, s32[2,512]{1,0:T(2,128)} %ids_ref.1, ...), custom_call_target="tpu_custom_call" | custom-call | tf_op jit(solution)/shard_map/layer/pallas_call | solution.py:700
  108.5 7.5 %adam.1 = (bf16[2,512,768]{2,1,0:T(8,128)(2,1)}, f32[2,512,768]{2,1,0:T(8,128)}, f32[1,1]{1,0:T(1,128)}, f32[3,96,192]{2,1,0:T(8,128)}, f32[3,96,192]{2,1,0:T(8,...) custom-call(bf16[2,512,768]{2,1,0:T(8,128)(2,1)} %get-tuple-element., ...), custom_call_target="tpu_custom_call" | custom-call | tf_op jit(solution)/shard_map/adam/pallas_call | solution.py:768
